TPU v7x, 256 devices: a whole 4x4x8 slice. The times are simulated.
256 devices in a mesh: layer: 2 (over z_hi), row: 16 (over y, x), col: 8 (over z_lo, core).
Axes of the slice: x: 4, y: 4, z: 8 (z_hi: 2, z_lo: 4; z = z_hi * 4 + z_lo), core: 2. Of those that a mesh axis runs over, the one named last changes fastest.
Arguments:
- root_rhs: float32 [32, 8, 1024], P(None, None, 'row'), may hold values from -6 to 6
- child_rhs: float32 [2, 32, 8, 1024], P('layer', None, None, 'row'), may hold values from -6 to 6
- root_factor: float32 [8, 8, 1024, 1024], P(None, None, 'row', 'col'), may hold values from -0.0625 to 0.0625
- child_factor: float32 [2, 8, 8, 1024, 1024], P('layer', None, None, 'row', 'col'), may hold values from -0.0625 to 0.0625
- coupling: float32 [2, 8, 8, 1024, 1024], P('layer', None, None, 'row', 'col'), may hold values from -0.0234375 to 0.0234375
- root_inverse: float32 [8, 1024, 1024], P(None, 'col', 'row'), as said below
- child_inverse: float32 [2, 8, 1024, 1024], P('layer', None, 'col', 'row'), as said below
Outputs:
- root_solution: float32 [32, 8, 1024], P(None, None, 'row')
- child_solution: float32 [2, 32, 8, 1024], P('layer', None, None, 'row')
Inputs may be any that keep to these rules, and one draw needn't show every extreme that they name: Each block of root_inverse is lower triangular. Each block of child_inverse is lower triangular.
All inputs are finite; a program needn't handle non-finite values.
Results may differ from a plain program's by a relative error of at most 0.00015.
Values sent between devices are 32-bit elements; how exact they have to be, the bound alone decides.
A program may use at most 64 MiB of HBM per device.

v0:
```python
import jax
import jax.numpy as jnp
from jax import lax
from jax.sharding import PartitionSpec as P

precise = lax.Precision.HIGHEST


def from_everyone(shard, axis):
    count = lax.axis_size(axis)
    return lax.all_to_all(
        jnp.broadcast_to(shard[None], (count, *shard.shape)), axis, 0, 0, tiled=True
    )


def of_everyone(shard, axis):
    return from_everyone(shard, axis).sum(axis=0)


def cut_along(shard, dim, count):
    before, after = (shard.shape[:dim], shard.shape[dim + 1 :])
    return jnp.moveaxis(shard.reshape(*before, count, -1, *after), dim, 0)


def sum_at_owner(shard, axis, dim):
    count = lax.axis_size(axis)
    blocks = lax.all_to_all(cut_along(shard, dim, count), axis, 0, 0, tiled=True)
    return jnp.sum(blocks, axis=0)


def pick(stack, index, axis):
    return lax.dynamic_index_in_dim(stack, index, axis, keepdims=False)


def forward(factor, inverse, right, extra, first_col):
    blocks = factor.shape[0]
    columns = right.shape[0]
    col_width = factor.shape[3]
    right_rows = jnp.transpose(right, (1, 0, 2))
    solved = jnp.zeros((blocks, columns, col_width), jnp.float32)

    def forward_step(target, solved):
        row_tiles = pick(factor, target, 0)
        partial_value = jnp.where(first_col, pick(right_rows, target, 0), 0.0) - pick(
            extra, target, 0
        )
        partial_value = partial_value - jnp.einsum(
            "jna,jba->nb", solved, row_tiles, precision=precise
        )
        residual = of_everyone(partial_value, "col")
        share = jnp.einsum("nb,ab->na", residual, pick(inverse, target, 0), precision=precise)
        solved_block = of_everyone(share, "row")
        return lax.dynamic_update_index_in_dim(solved, solved_block, target, 0)

    return lax.fori_loop(0, blocks, forward_step, solved)


def backward(factor, inverse, values, lowered, first_row):
    blocks = factor.shape[0]
    columns = values.shape[1]
    row_width = factor.shape[2]
    solved = jnp.zeros((blocks, columns, row_width), jnp.float32)

    def backward_step(step_at, solved):
        target = blocks - 1 - step_at
        column_tiles = pick(factor, target, 1)
        partial_value = jnp.where(first_row, pick(values, target, 0), 0.0) - pick(
            lowered, target, 0
        )
        partial_value = partial_value - jnp.einsum(
            "inb,iba->na", solved, column_tiles, precision=precise
        )
        pending = of_everyone(partial_value, "row")
        share = jnp.einsum("na,ab->nb", pending, pick(inverse, target, 0), precision=precise)
        solved_block = of_everyone(share, "col")
        return lax.dynamic_update_index_in_dim(solved, solved_block, target, 0)

    return lax.fori_loop(0, blocks, backward_step, solved)


def local(root_rhs, child_rhs, root_factor, child_factor, coupling, root_inverse, child_inverse):
    first_row = lax.axis_index("row") == 0
    first_col = lax.axis_index("col") == 0
    columns = root_rhs.shape[0]
    child_blocks = child_factor[0]
    child_inverses = child_inverse[0]
    couple_blocks = coupling[0]
    child_count = child_blocks.shape[0]
    root_count = root_factor.shape[0]
    row_width = root_factor.shape[2]
    col_width = root_factor.shape[3]
    child_down, root_down = (child_inverses, root_inverse)
    child_up, root_up = (child_inverses, root_inverse)
    child_start = jnp.zeros((child_count, columns, row_width), jnp.float32)
    child_forward = forward(child_blocks, child_down, child_rhs[0], child_start, first_col)
    lifted = jnp.einsum("jna,kjba->knb", child_forward, couple_blocks, precision=precise)
    lifted = sum_at_owner(lifted, "layer", 1)
    half_cols = lifted.shape[1]
    layer_index = lax.axis_index("layer")
    right_half = lax.dynamic_slice_in_dim(root_rhs, layer_index * half_cols, half_cols, 0)
    root_forward = forward(root_factor, root_down, right_half, lifted, first_col)
    empty = jnp.zeros((root_count, half_cols, col_width), jnp.float32)
    root_half = backward(root_factor, root_up, root_forward, empty, first_row)
    root_solved = lax.all_gather(root_half, "layer", axis=1, tiled=True)
    lowered = jnp.einsum("inb,ikba->kna", root_solved, couple_blocks, precision=precise)
    child_solved = backward(child_blocks, child_up, child_forward, lowered, first_row)
    root_solution = jnp.transpose(root_solved, (1, 0, 2))
    child_solution = jnp.transpose(child_solved, (1, 0, 2))[None]
    return (root_solution, child_solution)


def solution(mesh):
    in_specs = (
        P(None, None, "row"),
        P("layer", None, None, "row"),
        P(None, None, "row", "col"),
        P("layer", None, None, "row", "col"),
        P("layer", None, None, "row", "col"),
        P(None, "col", "row"),
        P("layer", None, "col", "row"),
    )
    out_specs = (P(None, None, "row"), P("layer", None, None, "row"))
    return jax.shard_map(local, mesh=mesh, in_specs=in_specs, out_specs=out_specs, check_vma=False)
```

profile of v0, /device:TPU:1, one launch (start us, length us, event | category | flops | bytes accessed | tf_op | source)
XLA Modules:
  0.0 823.3 jit_solution(13943321788043753610)
XLA Ops:
  6.1 202.5 %while.56 = (s32[]{:T(128)}, f32[8,32,128]{2,1,0:T(8,128)S(1)}, pred[]{:T(512)}, f32[8,32,64]{2,1,0:T(8,128)S(1)}, f32[8,8,64,128]{3,2,1,0:T(8,128)}, /*index=5*...) while((s32[]{:T(128)}, f32[8,32,128]{2,1,0:T(8,128)S(1)}, pred[]{:T(512)}, ...), condition=%wide.region_3.4_spmd, body=%wide.region_0.3_spmd.sunk | while | flops 28391424 | bytes 2557601 | solution.py:55
  7.6 12.3 %all_to_all.97 = f32[8,1,2048]{2,1,0:T(1,128)S(1)} all-to-all(f32[8,1,2048]{2,1,0:T(1,128)S(1)} %reshape.56), channel_id=1, replica_groups=mesh['layer'=2,'row'=16,'col'=8] {'col'}, dimensions={0} | all-to-all | bytes 131072 | tf_op jit(solution)/shard_map/while/body/eval_jaxpr/all_to_all | solution.py:11
  38.1 9.7 %all_to_all.97 = f32[8,1,2048]{2,1,0:T(1,128)S(1)} all-to-all(f32[8,1,2048]{2,1,0:T(1,128)S(1)} %reshape.56), channel_id=1, replica_groups=mesh['layer'=2,'row'=16,'col'=8] {'col'}, dimensions={0} | all-to-all | bytes 131072 | tf_op jit(solution)/shard_map/while/body/eval_jaxpr/all_to_all | solution.py:11
  226.6 192.5 %while.57 = (s32[]{:T(128)}, f32[8,16,128]{2,1,0:T(8,128)S(1)}, pred[]{:T(512)}, f32[8,16,64]{2,1,0:T(8,128)S(1)}, f32[8,16,64]{2,1,0:T(8,128)S(1)}, /*index=5*/...) while((s32[]{:T(128)}, f32[8,16,128]{2,1,0:T(8,128)S(1)}, pred[]{:T(512)}, ...), condition=%wide.region_8.9_spmd, body=%wide.region_5.8_spmd.sunk | while | flops 14196738 | bytes 1410729 | solution.py:55
  228.0 10.2 %all_to_all.98 = f32[8,1,1024]{2,1,0:T(1,128)S(1)} all-to-all(f32[8,1,1024]{2,1,0:T(1,128)S(1)} %reshape.58), channel_id=1, replica_groups=mesh['layer'=2,'row'=16,'col'=8] {'col'}, dimensions={0} | all-to-all | bytes 65536 | tf_op jit(solution)/shard_map/while/body/eval_jaxpr/all_to_all | solution.py:11
  252.9 9.3 %all_to_all.98 = f32[8,1,1024]{2,1,0:T(1,128)S(1)} all-to-all(f32[8,1,1024]{2,1,0:T(1,128)S(1)} %reshape.58), channel_id=1, replica_groups=mesh['layer'=2,'row'=16,'col'=8] {'col'}, dimensions={0} | all-to-all | bytes 65536 | tf_op jit(solution)/shard_map/while/body/eval_jaxpr/all_to_all | solution.py:11
  419.1 196.2 %while.58 = (s32[]{:T(128)}, f32[8,16,64]{2,1,0:T(8,128)S(1)}, pred[]{:T(512)}, f32[8,16,128]{2,1,0:T(8,128)S(1)}, f32[8,8,64,128]{3,2,1,0:T(8,128)}, /*index=5*...) while((s32[]{:T(128)}, f32[8,16,64]{2,1,0:T(8,128)S(1)}, ...), condition=%wide.region_12.13_spmd, body=%wide.region_9.12_spmd.sunk | while | flops 14197766 | bytes 1283807 | solution.py:78
  420.4 9.9 %all_to_all.99 = f32[16,16,128]{2,1,0:T(8,128)S(1)} all-to-all(f32[16,16,128]{2,1,0:T(8,128)S(1)} %broadcast_in_dim.251), channel_id=1, replica_groups=mesh['layer'=2,'row'=16,'col'=8] {'row'}, dimensions={0} | all-to-all | bytes 262144 | tf_op jit(solution)/shard_map/while/body/eval_jaxpr/all_to_all | solution.py:11
  445.9 9.7 %all_to_all.99 = f32[16,16,128]{2,1,0:T(8,128)S(1)} all-to-all(f32[16,16,128]{2,1,0:T(8,128)S(1)} %broadcast_in_dim.251), channel_id=1, replica_groups=mesh['layer'=2,'row'=16,'col'=8] {'row'}, dimensions={0} | all-to-all | bytes 262144 | tf_op jit(solution)/shard_map/while/body/eval_jaxpr/all_to_all | solution.py:11
  470.3 9.7 %all_to_all.99 = f32[16,16,128]{2,1,0:T(8,128)S(1)} all-to-all(f32[16,16,128]{2,1,0:T(8,128)S(1)} %broadcast_in_dim.251), channel_id=1, replica_groups=mesh['layer'=2,'row'=16,'col'=8] {'row'}, dimensions={0} | all-to-all | bytes 262144 | tf_op jit(solution)/shard_map/while/body/eval_jaxpr/all_to_all | solution.py:11
  494.7 9.7 %all_to_all.99 = f32[16,16,128]{2,1,0:T(8,128)S(1)} all-to-all(f32[16,16,128]{2,1,0:T(8,128)S(1)} %broadcast_in_dim.251), channel_id=1, replica_groups=mesh['layer'=2,'row'=16,'col'=8] {'row'}, dimensions={0} | all-to-all | bytes 262144 | tf_op jit(solution)/shard_map/while/body/eval_jaxpr/all_to_all | solution.py:11
  519.1 9.7 %all_to_all.99 = f32[16,16,128]{2,1,0:T(8,128)S(1)} all-to-all(f32[16,16,128]{2,1,0:T(8,128)S(1)} %broadcast_in_dim.251), channel_id=1, replica_groups=mesh['layer'=2,'row'=16,'col'=8] {'row'}, dimensions={0} | all-to-all | bytes 262144 | tf_op jit(solution)/shard_map/while/body/eval_jaxpr/all_to_all | solution.py:11
  543.5 9.7 %all_to_all.99 = f32[16,16,128]{2,1,0:T(8,128)S(1)} all-to-all(f32[16,16,128]{2,1,0:T(8,128)S(1)} %broadcast_in_dim.251), channel_id=1, replica_groups=mesh['layer'=2,'row'=16,'col'=8] {'row'}, dimensions={0} | all-to-all | bytes 262144 | tf_op jit(solution)/shard_map/while/body/eval_jaxpr/all_to_all | solution.py:11
  567.9 9.7 %all_to_all.99 = f32[16,16,128]{2,1,0:T(8,128)S(1)} all-to-all(f32[16,16,128]{2,1,0:T(8,128)S(1)} %broadcast_in_dim.251), channel_id=1, replica_groups=mesh['layer'=2,'row'=16,'col'=8] {'row'}, dimensions={0} | all-to-all | bytes 262144 | tf_op jit(solution)/shard_map/while/body/eval_jaxpr/all_to_all | solution.py:11
  592.3 9.7 %all_to_all.99 = f32[16,16,128]{2,1,0:T(8,128)S(1)} all-to-all(f32[16,16,128]{2,1,0:T(8,128)S(1)} %broadcast_in_dim.251), channel_id=1, replica_groups=mesh['layer'=2,'row'=16,'col'=8] {'row'}, dimensions={0} | all-to-all | bytes 262144 | tf_op jit(solution)/shard_map/while/body/eval_jaxpr/all_to_all | solution.py:11
  624.5 197.3 %while.59 = (s32[]{:T(128)}, f32[8,32,64]{2,1,0:T(8,128)S(1)}, pred[]{:T(512)}, f32[8,32,128]{2,1,0:T(8,128)S(1)}, f32[8,32,128]{2,1,0:T(8,128)S(1)}, /*index=5*...) while((s32[]{:T(128)}, f32[8,32,64]{2,1,0:T(8,128)S(1)}, ...), condition=%wide.region_16.17_spmd, body=%wide.region_13.16_spmd.sunk | while | flops 28399620 | bytes 2320103 | solution.py:78
  625.8 10.3 %all_to_all.100 = f32[16,32,128]{2,1,0:T(8,128)S(1)} all-to-all(f32[16,32,128]{2,1,0:T(8,128)S(1)} %broadcast_in_dim.254), channel_id=1, replica_groups=mesh['layer'=2,'row'=16,'col'=8] {'row'}, dimensions={0} | all-to-all | bytes 524288 | tf_op jit(solution)/shard_map/while/body/eval_jaxpr/all_to_all | solution.py:11
  651.5 10.2 %all_to_all.100 = f32[16,32,128]{2,1,0:T(8,128)S(1)} all-to-all(f32[16,32,128]{2,1,0:T(8,128)S(1)} %broadcast_in_dim.254), channel_id=1, replica_groups=mesh['layer'=2,'row'=16,'col'=8] {'row'}, dimensions={0} | all-to-all | bytes 524288 | tf_op jit(solution)/shard_map/while/body/eval_jaxpr/all_to_all | solution.py:11
  676.0 10.2 %all_to_all.100 = f32[16,32,128]{2,1,0:T(8,128)S(1)} all-to-all(f32[16,32,128]{2,1,0:T(8,128)S(1)} %broadcast_in_dim.254), channel_id=1, replica_groups=mesh['layer'=2,'row'=16,'col'=8] {'row'}, dimensions={0} | all-to-all | bytes 524288 | tf_op jit(solution)/shard_map/while/body/eval_jaxpr/all_to_all | solution.py:11
  700.5 10.2 %all_to_all.100 = f32[16,32,128]{2,1,0:T(8,128)S(1)} all-to-all(f32[16,32,128]{2,1,0:T(8,128)S(1)} %broadcast_in_dim.254), channel_id=1, replica_groups=mesh['layer'=2,'row'=16,'col'=8] {'row'}, dimensions={0} | all-to-all | bytes 524288 | tf_op jit(solution)/shard_map/while/body/eval_jaxpr/all_to_all | solution.py:11
  725.0 10.2 %all_to_all.100 = f32[16,32,128]{2,1,0:T(8,128)S(1)} all-to-all(f32[16,32,128]{2,1,0:T(8,128)S(1)} %broadcast_in_dim.254), channel_id=1, replica_groups=mesh['layer'=2,'row'=16,'col'=8] {'row'}, dimensions={0} | all-to-all | bytes 524288 | tf_op jit(solution)/shard_map/while/body/eval_jaxpr/all_to_all | solution.py:11
  749.5 10.2 %all_to_all.100 = f32[16,32,128]{2,1,0:T(8,128)S(1)} all-to-all(f32[16,32,128]{2,1,0:T(8,128)S(1)} %broadcast_in_dim.254), channel_id=1, replica_groups=mesh['layer'=2,'row'=16,'col'=8] {'row'}, dimensions={0} | all-to-all | bytes 524288 | tf_op jit(solution)/shard_map/while/body/eval_jaxpr/all_to_all | solution.py:11
  774.1 10.2 %all_to_all.100 = f32[16,32,128]{2,1,0:T(8,128)S(1)} all-to-all(f32[16,32,128]{2,1,0:T(8,128)S(1)} %broadcast_in_dim.254), channel_id=1, replica_groups=mesh['layer'=2,'row'=16,'col'=8] {'row'}, dimensions={0} | all-to-all | bytes 524288 | tf_op jit(solution)/shard_map/while/body/eval_jaxpr/all_to_all | solution.py:11
  798.6 10.2 %all_to_all.100 = f32[16,32,128]{2,1,0:T(8,128)S(1)} all-to-all(f32[16,32,128]{2,1,0:T(8,128)S(1)} %broadcast_in_dim.254), channel_id=1, replica_groups=mesh['layer'=2,'row'=16,'col'=8] {'row'}, dimensions={0} | all-to-all | bytes 524288 | tf_op jit(solution)/shard_map/while/body/eval_jaxpr/all_to_all | solution.py:11
  (454 shorter events, 619.6 us)
Async XLA Ops:
  22.2 14.3 %all-to-all-start.1 = ((f32[16,32,128]{2,1,0:T(8,128)}), f32[16,32,128]{2,1,0:T(8,128)S(1)}, u32[]{:S(2)}, u32[]{:S(2)}) async-start(f32[16,32,128]{2,1,0:T(8,128)} %broadcast_in_dim.246), calls=%async_computation.1 | async-start | bytes 524288 | tf_op jit(solution)/shard_map/while/body/eval_jaxpr/all_to_all | solution.py:11
  50.2 11.4 %all-to-all-start.1 = ((f32[16,32,128]{2,1,0:T(8,128)}), f32[16,32,128]{2,1,0:T(8,128)S(1)}, u32[]{:S(2)}, u32[]{:S(2)}) async-start(f32[16,32,128]{2,1,0:T(8,128)} %broadcast_in_dim.246), calls=%async_computation.1 | async-start | bytes 524288 | tf_op jit(solution)/shard_map/while/body/eval_jaxpr/all_to_all | solution.py:11
  74.7 11.4 %all-to-all-start.1 = ((f32[16,32,128]{2,1,0:T(8,128)}), f32[16,32,128]{2,1,0:T(8,128)S(1)}, u32[]{:S(2)}, u32[]{:S(2)}) async-start(f32[16,32,128]{2,1,0:T(8,128)} %broadcast_in_dim.246), calls=%async_computation.1 | async-start | bytes 524288 | tf_op jit(solution)/shard_map/while/body/eval_jaxpr/all_to_all | solution.py:11
  99.2 11.4 %all-to-all-start.1 = ((f32[16,32,128]{2,1,0:T(8,128)}), f32[16,32,128]{2,1,0:T(8,128)S(1)}, u32[]{:S(2)}, u32[]{:S(2)}) async-start(f32[16,32,128]{2,1,0:T(8,128)} %broadcast_in_dim.246), calls=%async_computation.1 | async-start | bytes 524288 | tf_op jit(solution)/shard_map/while/body/eval_jaxpr/all_to_all | solution.py:11
  123.7 11.4 %all-to-all-start.1 = ((f32[16,32,128]{2,1,0:T(8,128)}), f32[16,32,128]{2,1,0:T(8,128)S(1)}, u32[]{:S(2)}, u32[]{:S(2)}) async-start(f32[16,32,128]{2,1,0:T(8,128)} %broadcast_in_dim.246), calls=%async_computation.1 | async-start | bytes 524288 | tf_op jit(solution)/shard_map/while/body/eval_jaxpr/all_to_all | solution.py:11
  148.2 11.4 %all-to-all-start.1 = ((f32[16,32,128]{2,1,0:T(8,128)}), f32[16,32,128]{2,1,0:T(8,128)S(1)}, u32[]{:S(2)}, u32[]{:S(2)}) async-start(f32[16,32,128]{2,1,0:T(8,128)} %broadcast_in_dim.246), calls=%async_computation.1 | async-start | bytes 524288 | tf_op jit(solution)/shard_map/while/body/eval_jaxpr/all_to_all | solution.py:11
  172.7 11.4 %all-to-all-start.1 = ((f32[16,32,128]{2,1,0:T(8,128)}), f32[16,32,128]{2,1,0:T(8,128)S(1)}, u32[]{:S(2)}, u32[]{:S(2)}) async-start(f32[16,32,128]{2,1,0:T(8,128)} %broadcast_in_dim.246), calls=%async_computation.1 | async-start | bytes 524288 | tf_op jit(solution)/shard_map/while/body/eval_jaxpr/all_to_all | solution.py:11
  197.2 11.4 %all-to-all-start.1 = ((f32[16,32,128]{2,1,0:T(8,128)}), f32[16,32,128]{2,1,0:T(8,128)S(1)}, u32[]{:S(2)}, u32[]{:S(2)}) async-start(f32[16,32,128]{2,1,0:T(8,128)} %broadcast_in_dim.246), calls=%async_computation.1 | async-start | bytes 524288 | tf_op jit(solution)/shard_map/while/body/eval_jaxpr/all_to_all | solution.py:11
  212.4 12.7 %all-to-all-start.8 = ((f32[2,1,8192]{2,1,0:T(1,128)}), f32[2,1,8192]{2,1,0:T(1,128)S(1)}, u32[]{:S(2)}, u32[]{:S(2)}) async-start(f32[2,1,8192]{2,1,0:T(1,128)} %reshape.46), calls=%async_computation.8 | async-start | bytes 131072 | tf_op jit(solution)/shard_map/all_to_all | solution.py:27
  432.0 11.3 %all-to-all-start.5 = ((f32[8,1,1024]{2,1,0:T(1,128)}), f32[8,1,1024]{2,1,0:T(1,128)S(1)}, u32[]{:S(2)}, u32[]{:S(2)}) async-start(f32[8,1,1024]{2,1,0:T(1,128)} %reshape.60), calls=%async_computation.5 | async-start | bytes 65536 | tf_op jit(solution)/shard_map/while/body/eval_jaxpr/all_to_all | solution.py:11
  457.3 10.4 %all-to-all-start.5 = ((f32[8,1,1024]{2,1,0:T(1,128)}), f32[8,1,1024]{2,1,0:T(1,128)S(1)}, u32[]{:S(2)}, u32[]{:S(2)}) async-start(f32[8,1,1024]{2,1,0:T(1,128)} %reshape.60), calls=%async_computation.5 | async-start | bytes 65536 | tf_op jit(solution)/shard_map/while/body/eval_jaxpr/all_to_all | solution.py:11
  481.7 10.4 %all-to-all-start.5 = ((f32[8,1,1024]{2,1,0:T(1,128)}), f32[8,1,1024]{2,1,0:T(1,128)S(1)}, u32[]{:S(2)}, u32[]{:S(2)}) async-start(f32[8,1,1024]{2,1,0:T(1,128)} %reshape.60), calls=%async_computation.5 | async-start | bytes 65536 | tf_op jit(solution)/shard_map/while/body/eval_jaxpr/all_to_all | solution.py:11
  506.1 10.4 %all-to-all-start.5 = ((f32[8,1,1024]{2,1,0:T(1,128)}), f32[8,1,1024]{2,1,0:T(1,128)S(1)}, u32[]{:S(2)}, u32[]{:S(2)}) async-start(f32[8,1,1024]{2,1,0:T(1,128)} %reshape.60), calls=%async_computation.5 | async-start | bytes 65536 | tf_op jit(solution)/shard_map/while/body/eval_jaxpr/all_to_all | solution.py:11
  530.5 10.4 %all-to-all-start.5 = ((f32[8,1,1024]{2,1,0:T(1,128)}), f32[8,1,1024]{2,1,0:T(1,128)S(1)}, u32[]{:S(2)}, u32[]{:S(2)}) async-start(f32[8,1,1024]{2,1,0:T(1,128)} %reshape.60), calls=%async_computation.5 | async-start | bytes 65536 | tf_op jit(solution)/shard_map/while/body/eval_jaxpr/all_to_all | solution.py:11
  554.9 10.4 %all-to-all-start.5 = ((f32[8,1,1024]{2,1,0:T(1,128)}), f32[8,1,1024]{2,1,0:T(1,128)S(1)}, u32[]{:S(2)}, u32[]{:S(2)}) async-start(f32[8,1,1024]{2,1,0:T(1,128)} %reshape.60), calls=%async_computation.5 | async-start | bytes 65536 | tf_op jit(solution)/shard_map/while/body/eval_jaxpr/all_to_all | solution.py:11
  579.2 10.4 %all-to-all-start.5 = ((f32[8,1,1024]{2,1,0:T(1,128)}), f32[8,1,1024]{2,1,0:T(1,128)S(1)}, u32[]{:S(2)}, u32[]{:S(2)}) async-start(f32[8,1,1024]{2,1,0:T(1,128)} %reshape.60), calls=%async_computation.5 | async-start | bytes 65536 | tf_op jit(solution)/shard_map/while/body/eval_jaxpr/all_to_all | solution.py:11
  637.1 11.6 %all-to-all-start.7 = ((f32[8,1,2048]{2,1,0:T(1,128)}), f32[8,1,2048]{2,1,0:T(1,128)S(1)}, u32[]{:S(2)}, u32[]{:S(2)}) async-start(f32[8,1,2048]{2,1,0:T(1,128)} %reshape.62), calls=%async_computation.7 | async-start | bytes 131072 | tf_op jit(solution)/shard_map/while/body/eval_jaxpr/all_to_all | solution.py:11
  662.6 10.6 %all-to-all-start.7 = ((f32[8,1,2048]{2,1,0:T(1,128)}), f32[8,1,2048]{2,1,0:T(1,128)S(1)}, u32[]{:S(2)}, u32[]{:S(2)}) async-start(f32[8,1,2048]{2,1,0:T(1,128)} %reshape.62), calls=%async_computation.7 | async-start | bytes 131072 | tf_op jit(solution)/shard_map/while/body/eval_jaxpr/all_to_all | solution.py:11
  687.2 10.6 %all-to-all-start.7 = ((f32[8,1,2048]{2,1,0:T(1,128)}), f32[8,1,2048]{2,1,0:T(1,128)S(1)}, u32[]{:S(2)}, u32[]{:S(2)}) async-start(f32[8,1,2048]{2,1,0:T(1,128)} %reshape.62), calls=%async_computation.7 | async-start | bytes 131072 | tf_op jit(solution)/shard_map/while/body/eval_jaxpr/all_to_all | solution.py:11
  711.7 10.6 %all-to-all-start.7 = ((f32[8,1,2048]{2,1,0:T(1,128)}), f32[8,1,2048]{2,1,0:T(1,128)S(1)}, u32[]{:S(2)}, u32[]{:S(2)}) async-start(f32[8,1,2048]{2,1,0:T(1,128)} %reshape.62), calls=%async_computation.7 | async-start | bytes 131072 | tf_op jit(solution)/shard_map/while/body/eval_jaxpr/all_to_all | solution.py:11
  736.2 10.6 %all-to-all-start.7 = ((f32[8,1,2048]{2,1,0:T(1,128)}), f32[8,1,2048]{2,1,0:T(1,128)S(1)}, u32[]{:S(2)}, u32[]{:S(2)}) async-start(f32[8,1,2048]{2,1,0:T(1,128)} %reshape.62), calls=%async_computation.7 | async-start | bytes 131072 | tf_op jit(solution)/shard_map/while/body/eval_jaxpr/all_to_all | solution.py:11
  760.7 10.6 %all-to-all-start.7 = ((f32[8,1,2048]{2,1,0:T(1,128)}), f32[8,1,2048]{2,1,0:T(1,128)S(1)}, u32[]{:S(2)}, u32[]{:S(2)}) async-start(f32[8,1,2048]{2,1,0:T(1,128)} %reshape.62), calls=%async_computation.7 | async-start | bytes 131072 | tf_op jit(solution)/shard_map/while/body/eval_jaxpr/all_to_all | solution.py:11
  785.2 10.6 %all-to-all-start.7 = ((f32[8,1,2048]{2,1,0:T(1,128)}), f32[8,1,2048]{2,1,0:T(1,128)S(1)}, u32[]{:S(2)}, u32[]{:S(2)}) async-start(f32[8,1,2048]{2,1,0:T(1,128)} %reshape.62), calls=%async_computation.7 | async-start | bytes 131072 | tf_op jit(solution)/shard_map/while/body/eval_jaxpr/all_to_all | solution.py:11
  809.7 10.6 %all-to-all-start.7 = ((f32[8,1,2048]{2,1,0:T(1,128)}), f32[8,1,2048]{2,1,0:T(1,128)S(1)}, u32[]{:S(2)}, u32[]{:S(2)}) async-start(f32[8,1,2048]{2,1,0:T(1,128)} %reshape.62), calls=%async_computation.7 | async-start | bytes 131072 | tf_op jit(solution)/shard_map/while/body/eval_jaxpr/all_to_all | solution.py:11
  (11 other events, 310.2 us)
where the time goes:
time: 830 us; the launch traced here: 823 us
  blocking collectives  319 us (38%)
  waiting for transfers between devices  205 us (25%)
  starting transfers between devices  154 us (19%)
  matrix products  61.4 us (7%)
  local copies, waits for them, and re-layouts  54.1 us (7%)
  other arithmetic  26.3 us (3%)
    all_to_all x32, blocking collectives, from_everyone(): lax.all_to_all(jnp.broadcast_to(shard[None], (count, *shard.shape)), axis...  311 us
    all_to_all x32, waiting for transfers between devices, from_everyone(): lax.all_to_all(jnp.broadcast_to(shard[None], (count, *shard.shape)), axis...  198 us
    all_to_all x32, starting transfers between devices, from_everyone(): lax.all_to_all(jnp.broadcast_to(shard[None], (count, *shard.shape)), axis...  149 us
    all_to_all x32, other arithmetic, from_everyone(): lax.all_to_all(jnp.broadcast_to(shard[None], (count, *shard.shape)), axis...  24.3 us
    dot_general x16, matrix products, forward_step(): jnp.einsum('jna,jba->nb', solved, row_tiles, precision=precise)  20.2 us
    dot_general x16, matrix products, backward_step(): jnp.einsum('inb,iba->na', solved, column_tiles, precision=precise)  19.8 us
  transfers between devices with their start and end apart: 33, of which 33 were waited for; matrix products, arithmetic and copies ran while one was open for 0% of the time, Pallas kernels for 0%

commit v1 on v0

v1 whole, which is shorter than its diff:
```python
import jax
import jax.numpy as jnp
from jax import lax
from jax.experimental import pallas as pl
from jax.experimental.pallas import tpu as pltpu
from jax.sharding import PartitionSpec as P

MESH = pl.DeviceIdType.MESH
BLOCKS = 8
ROWS = 16
COLS = 8


def dot_t(x, y):
    return lax.dot_general(
        x, y, (((1,), (1,)), ((), ())), precision=lax.Precision.HIGHEST,
        preferred_element_type=jnp.float32,
    )


def dot_n(x, y):
    return lax.dot_general(
        x, y, (((1,), (0,)), ((), ())), precision=lax.Precision.HIGHEST,
        preferred_element_type=jnp.float32,
    )


def pack(x):
    half = x.shape[0] // 2
    return jnp.concatenate([x[:half], x[half:]], axis=1)


def unpack(x):
    half = x.shape[1] // 2
    return jnp.concatenate([x[:, :half], x[:, half:]], axis=0)


def kernel(
    root_rhs, child_rhs, root_factor, child_factor, coupling, root_inv, child_inv,
    root_out, child_out,
    u_ref, v_ref, s_half, acc, col_buf, row_buf, lift_buf, lift_in, s_in,
    col_send, col_recv, row_send, row_recv, pair_send, pair_recv, s_send, s_recv,
):
    layer = lax.axis_index("layer")
    row = lax.axis_index("row")
    col = lax.axis_index("col")
    other = (1 - layer, row, col)
    col_peers = [lax.rem(col + k, COLS) for k in range(1, COLS)]
    row_peers = [lax.rem(row + k, ROWS) for k in range(1, ROWS)]

    barrier = pltpu.get_barrier_semaphore()
    for peer in col_peers:
        pl.semaphore_signal(barrier, inc=1, device_id=(layer, row, peer), device_id_type=MESH)
    for peer in row_peers:
        pl.semaphore_signal(barrier, inc=1, device_id=(layer, peer, col), device_id_type=MESH)
    pl.semaphore_signal(barrier, inc=1, device_id=other, device_id_type=MESH)
    acc[...] = jnp.zeros_like(acc)
    pl.semaphore_wait(barrier, COLS + ROWS - 1)

    def col_copy(par, slot, at, height, peer):
        return pltpu.make_async_remote_copy(
            src_ref=col_buf.at[par, slot, pl.ds(0, height)],
            dst_ref=col_buf.at[par, slot, pl.ds(0, height)],
            send_sem=col_send.at[par, at],
            recv_sem=col_recv.at[par, slot],
            device_id=(layer, row, peer),
            device_id_type=MESH,
        )

    def row_copy(par, slot, at, height, peer):
        return pltpu.make_async_remote_copy(
            src_ref=row_buf.at[par, slot, pl.ds(0, height)],
            dst_ref=row_buf.at[par, slot, pl.ds(0, height)],
            send_sem=row_send.at[par, at],
            recv_sem=row_recv.at[par, slot],
            device_id=(layer, peer, col),
            device_id_type=MESH,
        )

    def over_col(par, value, beside):
        packed = pack(value)
        height = packed.shape[0]
        col_buf[par, col, 0:height] = packed
        for at, peer in enumerate(col_peers):
            col_copy(par, col, at, height, peer).start()
        beside()
        for at, peer in enumerate(col_peers):
            col_copy(par, peer, at, height, peer).wait_recv()
        total = col_buf[par, 0, 0:height]
        for slot in range(1, COLS):
            total = total + col_buf[par, slot, 0:height]
        for at, peer in enumerate(col_peers):
            col_copy(par, col, at, height, peer).wait_send()
        return unpack(total)

    def over_row(par, value, beside):
        height = value.shape[0]
        row_buf[par, row, 0:height] = value
        for at, peer in enumerate(row_peers):
            row_copy(par, row, at, height, peer).start()
        beside()
        for at, peer in enumerate(row_peers):
            row_copy(par, peer, at, height, peer).wait_recv()
        total = row_buf[par, 0, 0:height]
        for slot in range(1, ROWS):
            total = total + row_buf[par, slot, 0:height]
        for at, peer in enumerate(row_peers):
            row_copy(par, row, at, height, peer).wait_send()
        return total

    nrhs = child_rhs.shape[1]
    half = nrhs // 2
    mine = layer * half
    theirs = (1 - layer) * half

    def child_forward(k, carry):
        par = lax.rem(k, 2)
        before = jnp.maximum(k - 1, 0)

        def trailing():
            value = u_ref[before]

            @pl.loop(k + 1, BLOCKS)
            def _(later):
                @pl.when(k > 0)
                def _():
                    acc[later, :, 0:64] += dot_t(value, child_factor[later, before])

        def lifting():
            @pl.when(k > 0)
            def _():
                value = u_ref[before]

                @pl.loop(0, BLOCKS)
                def _(at):
                    lift_buf[at] += dot_t(value, coupling[at, before])

        pending = child_rhs[k] - over_col(par, acc[k, :, 0:64], trailing)
        value = over_row(par, dot_t(pending, child_inv[k]), lifting)
        u_ref[k] = value
        after = jnp.minimum(k + 1, BLOCKS - 1)

        @pl.when(k < BLOCKS - 1)
        def _():
            acc[after, :, 0:64] += dot_t(value, child_factor[after, k])

        return carry

    lift_buf[...] = jnp.zeros_like(lift_buf)
    lax.fori_loop(0, BLOCKS, child_forward, 0)
    last = u_ref[BLOCKS - 1]
    for at in range(BLOCKS):
        lift_buf[at] += dot_t(last, coupling[at, BLOCKS - 1])
    lift_copy = pltpu.make_async_remote_copy(
        src_ref=lift_buf.at[:, pl.ds(theirs, half)],
        dst_ref=lift_in,
        send_sem=pair_send,
        recv_sem=pair_recv,
        device_id=other,
        device_id_type=MESH,
    )
    lift_copy.start()
    lift_copy.wait_recv()
    for at in range(BLOCKS):
        acc[at, 0:half, 0:64] = lift_buf[at, pl.ds(mine, half)] + lift_in[at]
    lift_copy.wait_send()

    def root_forward(k, carry):
        par = lax.rem(k, 2)
        before = jnp.maximum(k - 1, 0)

        def trailing():
            value = v_ref[before]

            @pl.loop(k + 1, BLOCKS)
            def _(later):
                @pl.when(k > 0)
                def _():
                    acc[later, 0:half, 0:64] += dot_t(value, root_factor[later, before])

        pending = root_rhs[k, pl.ds(mine, half)] - over_col(par, acc[k, 0:half, 0:64], trailing)
        value = over_row(par, dot_t(pending, root_inv[k]), lambda: None)
        v_ref[k] = value
        after = jnp.minimum(k + 1, BLOCKS - 1)

        @pl.when(k < BLOCKS - 1)
        def _():
            acc[after, 0:half, 0:64] += dot_t(value, root_factor[after, k])

        return carry

    lax.fori_loop(0, BLOCKS, root_forward, 0)

    acc[...] = jnp.zeros_like(acc)

    def s_copy(k):
        return pltpu.make_async_remote_copy(
            src_ref=s_half.at[k],
            dst_ref=s_in.at[k],
            send_sem=s_send.at[k],
            recv_sem=s_recv.at[k],
            device_id=other,
            device_id_type=MESH,
        )

    def root_backward(step, carry):
        par = lax.rem(step, 2)
        k = BLOCKS - 1 - step
        after = jnp.minimum(k + 1, BLOCKS - 1)

        def trailing():
            value = s_half[after]

            @pl.loop(0, k)
            def _(earlier):
                @pl.when(step > 0)
                def _():
                    acc[earlier, 0:half] += dot_n(value, root_factor[after, earlier])

        pending = v_ref[k] - over_row(par, acc[k, 0:half], trailing)
        value = over_col(par, dot_n(pending, root_inv[k]), lambda: None)
        s_half[k] = value
        s_copy(k).start()
        before = jnp.maximum(k - 1, 0)

        @pl.when(k > 0)
        def _():
            acc[before, 0:half] += dot_n(value, root_factor[k, before])

        return carry

    lax.fori_loop(0, BLOCKS, root_backward, 0)

    acc[...] = jnp.zeros_like(acc)

    @pl.loop(0, BLOCKS)
    def _(step):
        k = BLOCKS - 1 - step
        s_copy(k).wait_recv()
        root_out[k, pl.ds(mine, half)] = s_half[k]
        root_out[k, pl.ds(theirs, half)] = s_in[k]
        value = root_out[k]

        @pl.loop(0, BLOCKS)
        def _(at):
            acc[at] += dot_n(value, coupling[k, at])

        s_copy(k).wait_send()

    def child_backward(step, carry):
        par = lax.rem(step, 2)
        k = BLOCKS - 1 - step
        after = jnp.minimum(k + 1, BLOCKS - 1)

        def trailing():
            value = child_out[after]

            @pl.loop(0, k)
            def _(earlier):
                @pl.when(step > 0)
                def _():
                    acc[earlier] += dot_n(value, child_factor[after, earlier])

        pending = u_ref[k] - over_row(par, acc[k], trailing)
        value = over_col(par, dot_n(pending, child_inv[k]), lambda: None)
        child_out[k] = value
        before = jnp.maximum(k - 1, 0)

        @pl.when(k > 0)
        def _():
            acc[before] += dot_n(value, child_factor[k, before])

        return carry

    lax.fori_loop(0, BLOCKS, child_backward, 0)


def local(root_rhs, child_rhs, root_factor, child_factor, coupling, root_inverse, child_inverse):
    nrhs = root_rhs.shape[0]
    half = nrhs // 2
    wide, thin = root_factor.shape[3], root_factor.shape[2]
    vmem = pl.BlockSpec(memory_space=pltpu.VMEM)
    f32 = jnp.float32
    dma = pltpu.SemaphoreType.DMA
    root, child = pl.pallas_call(
        kernel,
        out_shape=(
            jax.ShapeDtypeStruct((BLOCKS, nrhs, thin), f32),
            jax.ShapeDtypeStruct((BLOCKS, nrhs, thin), f32),
        ),
        in_specs=[vmem] * 7,
        out_specs=[vmem] * 2,
        scratch_shapes=[
            pltpu.VMEM((BLOCKS, nrhs, wide), f32),
            pltpu.VMEM((BLOCKS, half, wide), f32),
            pltpu.VMEM((BLOCKS, half, thin), f32),
            pltpu.VMEM((BLOCKS, nrhs, wide), f32),
            pltpu.VMEM((2, COLS, half, wide), f32),
            pltpu.VMEM((2, ROWS, nrhs, wide), f32),
            pltpu.VMEM((BLOCKS, nrhs, thin), f32),
            pltpu.VMEM((BLOCKS, half, thin), f32),
            pltpu.VMEM((BLOCKS, half, thin), f32),
            dma((2, COLS)), dma((2, COLS)), dma((2, ROWS)), dma((2, ROWS)),
            dma, dma, dma((BLOCKS,)), dma((BLOCKS,)),
        ],
        compiler_params=pltpu.CompilerParams(
            collective_id=0, has_side_effects=True, vmem_limit_bytes=48 << 20
        ),
    )(
        jnp.transpose(root_rhs, (1, 0, 2)),
        jnp.transpose(child_rhs[0], (1, 0, 2)),
        root_factor, child_factor[0], coupling[0], root_inverse, child_inverse[0],
    )
    return jnp.transpose(root, (1, 0, 2)), jnp.transpose(child, (1, 0, 2))[None]


def solution(mesh):
    in_specs = (
        P(None, None, "row"),
        P("layer", None, None, "row"),
        P(None, None, "row", "col"),
        P("layer", None, None, "row", "col"),
        P("layer", None, None, "row", "col"),
        P(None, "col", "row"),
        P("layer", None, "col", "row"),
    )
    out_specs = (P(None, None, "row"), P("layer", None, None, "row"))
    return jax.shard_map(local, mesh=mesh, in_specs=in_specs, out_specs=out_specs, check_vma=False)
```

time: 830 us -> 352 us (0.42)
  Pallas kernels: 0 us -> 344 us
  blocking collectives: 319 us -> 0 us
  waiting for transfers between devices: 205 us -> 0 us
  starting transfers between devices: 154 us -> 0 us
  matrix products: 61.4 us -> 0 us
  local copies, waits for them, and re-layouts: 54.1 us -> 7.38 us
  other arithmetic: 26.3 us -> 0 us
    pallas_call x0 -> x1, Pallas kernels: none -> 344 us  [local(): pl.pallas_call(kernel, out_shape=(jax.ShapeDtypeStruct((BLOCKS, nrhs, thi...]
    all_to_all x32 -> x0, blocking collectives: 311 us -> none  [from_everyone(): lax.all_to_all(jnp.broadcast_to(shard[None], (count, *shard.shape)), axis...]
    all_to_all x33 -> x0, waiting for transfers between devices: 205 us -> none  [the longest x32 198 us: from_everyone(): lax.all_to_all(jnp.broadcast_to(shard[None], (count, *shard.shape)), axis...]
    all_to_all x33 -> x0, starting transfers between devices: 154 us -> none  [the longest x32 149 us: from_everyone(): lax.all_to_all(jnp.broadcast_to(shard[None], (count, *shard.shape)), axis...]
    dot_general x66 -> x0, matrix products: 61.4 us -> none  [the longest x16 20.2 us: forward_step(): jnp.einsum('jna,jba->nb', solved, row_tiles, precision=precise)]
    all_to_all x33 -> x0, other arithmetic: 25.1 us -> none  [the longest x32 24.3 us: from_everyone(): lax.all_to_all(jnp.broadcast_to(shard[None], (count, *shard.shape)), axis...]
    while x65 -> x0, local copies, waits for them, and re-layouts: 16.9 us -> none
    all_to_all x33 -> x0, local copies, waits for them, and re-layouts: 16.9 us -> none  [the longest x32 16.4 us: from_everyone(): lax.all_to_all(jnp.broadcast_to(shard[None], (count, *shard.shape)), axis...]
  transfers between devices with their start and end apart: 33 -> 0, of which waited for: 33 -> 0; matrix products, arithmetic and copies ran while one was open for 0% -> 0% of each run, Pallas kernels for 0% -> 0%
where the time goes in v1:
time: 352 us
  Pallas kernels  344 us (98%)
  local copies, waits for them, and re-layouts  7.38 us (2%)
    pallas_call x1, Pallas kernels, local(): pl.pallas_call(kernel, out_shape=(jax.ShapeDtypeStruct((BLOCKS, nrhs, thi...  344 us
    unnamed x10, local copies, waits for them, and re-layouts  7.38 us

profile of v1, /device:TPU:1, one launch (start us, length us, event | category | flops | bytes accessed | tf_op | source)
XLA Modules:
  0.0 351.9 jit_solution(13370341680348722477)
XLA Ops:
  0.6 0.0 copy-start
  0.6 1.1 copy.18
  1.7 0.9 copy.17
  2.7 1.2 copy.12.root_inv
  3.8 1.2 copy.11
  5.0 0.0 copy-done
  5.0 0.0 copy-start.1
  5.0 1.6 copy-done.1
  6.6 343.9 %shard_map.86 = (f32[8,32,64]{2,1,0:T(8,128)S(1)}, f32[8,32,64]{2,1,0:T(8,128)S(1)}) custom-call(f32[8,32,64]{2,1,0:T(8,128)S(1)} %bitcast.17, f32[8,32,64]{2,1,0:T(8,128)S(1)} %bitcast.18, f32[8,8,64,128]{3,2,1,0:T(8,128)S(1)} %copy-done, f32[8,8,64,128]{3,2,1,0:T(8,128)S(1)} %bitcast.15, f32[8,8,64,128]{3,2,1,0:T(8,128)} %bitcast.21, ...), custom_call_target="tpu_custom_call" | custom-call | tf_op jit(solution)/shard_map/pallas_call | solution.py:285
  350.4 0.7 copy.13
  351.2 0.7 copy.14
Async XLA Ops:
  0.6 4.3 %copy-start = (f32[8,8,64,128]{3,2,1,0:T(8,128)S(1)}, f32[8,8,64,128]{3,2,1,0:T(8,128)}, u32[]{:S(2)}) copy-start(f32[8,8,64,128]{3,2,1,0:T(8,128)} %root_factor.1) | copy-start | bytes 6291460
  5.0 1.6 copy-start.1

commit v2 on v0

v2 whole, which is shorter than its diff:
```python
import jax
import jax.numpy as jnp
from jax import lax
from jax.experimental import pallas as pl
from jax.experimental.pallas import tpu as pltpu
from jax.sharding import PartitionSpec as P

MESH = pl.DeviceIdType.MESH
PAIRS = 4
ROWS = 16
COLS = 8
THIN = 64
WIDE = 128
SINGLES = 4


def dot_t(x, y):
    return lax.dot_general(
        x, y, (((1,), (1,)), ((), ())), precision=lax.Precision.HIGHEST,
        preferred_element_type=jnp.float32,
    )


def dot_n(x, y):
    return lax.dot_general(
        x, y, (((1,), (0,)), ((), ())), precision=lax.Precision.HIGHEST,
        preferred_element_type=jnp.float32,
    )


def pack(x):
    half = x.shape[0] // 2
    return jnp.concatenate([x[:half], x[half:]], axis=1)


def unpack(x):
    half = x.shape[1] // 2
    return jnp.concatenate([x[:, :half], x[:, half:]], axis=0)


def pair_rows(ref, pair, block):
    return ref[pl.ds(2 * pair, 2), block].reshape(2 * THIN, WIDE)


def kernel(
    root_rhs, child_rhs, root_factor, child_factor, coupling, root_wt, child_wt,
    root_out, child_out,
    u_ref, v_ref, s_half, s_in, acc_f, acc_r, acc_b, acc_c, superw,
    col_buf, row_buf, lift_buf, lift_in, a0_buf, c_buf, a1_buf, t_buf, x_buf,
    col_send, col_recv, row_send, row_recv, lift_send, lift_recv, s_send, s_recv,
    team_send, team_recv, t_send, t_recv, x_send, x_recv,
):
    layer = lax.axis_index("layer")
    row = lax.axis_index("row")
    col = lax.axis_index("col")
    other = (1 - layer, row, col)
    col_peers = [lax.rem(col + k, COLS) for k in range(1, COLS)]
    row_peers = [lax.rem(row + k, ROWS) for k in range(1, ROWS)]
    row4, rowm = row // 4, lax.rem(row, 4)
    col2, colm = col // 2, lax.rem(col, 2)
    nrhs = child_rhs.shape[1]
    half = nrhs // 2
    mine = pl.multiple_of(layer * half, half)
    theirs = pl.multiple_of((1 - layer) * half, half)

    barrier = pltpu.get_barrier_semaphore()
    for peer in col_peers:
        pl.semaphore_signal(barrier, inc=1, device_id=(layer, row, peer), device_id_type=MESH)
    for peer in row_peers:
        pl.semaphore_signal(barrier, inc=1, device_id=(layer, peer, col), device_id_type=MESH)
    pl.semaphore_signal(barrier, inc=1, device_id=other, device_id_type=MESH)
    for ref in (acc_f, acc_b, acc_c, lift_buf):
        ref[...] = jnp.zeros_like(ref)
    pl.semaphore_wait(barrier, COLS + ROWS - 1)

    def col_copy(par, slot, at, height, peer):
        where = col_buf.at[par, slot, pl.ds(0, height)]
        return pltpu.make_async_remote_copy(
            src_ref=where, dst_ref=where,
            send_sem=col_send.at[par, at], recv_sem=col_recv.at[par, slot],
            device_id=(layer, row, peer), device_id_type=MESH,
        )

    def row_copy(par, slot, at, height, width, peer):
        where = row_buf.at[par, slot, pl.ds(0, height), pl.ds(0, width)]
        return pltpu.make_async_remote_copy(
            src_ref=where, dst_ref=where,
            send_sem=row_send.at[par, at], recv_sem=row_recv.at[par, slot],
            device_id=(layer, peer, col), device_id_type=MESH,
        )

    def over_col(par, value, beside):
        height = value.shape[0]
        col_buf[par, col, 0:height] = value
        for at, peer in enumerate(col_peers):
            col_copy(par, col, at, height, peer).start()
        beside()
        for at, peer in enumerate(col_peers):
            col_copy(par, peer, at, height, peer).wait_recv()
        total = col_buf[par, 0, 0:height]
        for slot in range(1, COLS):
            total = total + col_buf[par, slot, 0:height]
        for at, peer in enumerate(col_peers):
            col_copy(par, col, at, height, peer).wait_send()
        return total

    def over_row(par, value, beside):
        height, width = value.shape
        row_buf[par, row, 0:height, 0:width] = value
        for at, peer in enumerate(row_peers):
            row_copy(par, row, at, height, width, peer).start()
        beside()
        for at, peer in enumerate(row_peers):
            row_copy(par, peer, at, height, width, peer).wait_recv()
        total = row_buf[par, 0, 0:height, 0:width]
        for slot in range(1, ROWS):
            total = total + row_buf[par, slot, 0:height, 0:width]
        for at, peer in enumerate(row_peers):
            row_copy(par, row, at, height, width, peer).wait_send()
        return total

    def placed(src, dst, recv, send, to_row, to_col, wanted, finish):
        here = jnp.logical_and(to_row == row, to_col == col)

        @pl.when(jnp.logical_and(wanted, jnp.logical_not(here)))
        def _():
            copy = pltpu.make_async_remote_copy(
                src_ref=src, dst_ref=dst, send_sem=send, recv_sem=recv,
                device_id=(layer, to_row, to_col), device_id_type=MESH,
            )
            copy.wait_send() if finish else copy.start()

        if not finish:
            @pl.when(jnp.logical_and(wanted, here))
            def _():
                pltpu.make_async_copy(src, dst, recv).start()

    def to_team(base, wt, factor, finish=False):
        @pl.loop(0, PAIRS)
        def _(turn):
            pair = lax.rem(turn + col, PAIRS)
            team = base + pair
            for j in range(4):
                placed(
                    wt.at[2 * pair], a0_buf.at[col, rowm], team_recv.at[0],
                    team_send.at[team, j], 4 * row4 + j, team, col2 >= row4, finish,
                )
            for i in range(4):
                placed(
                    factor.at[2 * pair + 1, 2 * pair], c_buf.at[col, rowm], team_recv.at[1],
                    team_send.at[team, 4 + i], 4 * i + row4, team, col2 >= i, finish,
                )
            for i in range(4):
                placed(
                    wt.at[2 * pair + 1], a1_buf.at[row, colm], team_recv.at[2],
                    team_send.at[team, 8 + i], 4 * i + col2, team, row4 <= col2, finish,
                )

    def arrived(ref, sem):
        pltpu.make_async_copy(ref, ref, sem).wait()

    def t_copy(slot, at, to):
        return pltpu.make_async_remote_copy(
            src_ref=t_buf.at[slot], dst_ref=t_buf.at[slot],
            send_sem=t_send.at[at], recv_sem=t_recv.at[slot],
            device_id=(layer, 4 * row4 + to, col), device_id_type=MESH,
        )

    def team_first():
        for part in range(4):
            @pl.when(row4 == part)
            def _():
                arrived(a0_buf.at[pl.ds(2 * part, COLS - 2 * part)], team_recv.at[0])
                arrived(c_buf.at[pl.ds(2 * part, COLS - 2 * part)], team_recv.at[1])
        t_buf[rowm] = jnp.zeros((4 * THIN, 4 * THIN), jnp.float32)

        @pl.loop(2 * row4, COLS)
        def _(at):
            t_buf[rowm] += dot_t(
                a0_buf[at].reshape(4 * THIN, WIDE), c_buf[at].reshape(4 * THIN, WIDE)
            )

        for to in range(1, 4):
            @pl.when(to > rowm)
            def _():
                t_copy(rowm, to, to).start()

    def team_second(start):
        if start:
            for part in range(4):
                @pl.when(rowm == part)
                def _():
                    arrived(a1_buf.at[pl.ds(0, 4 * part + 4)], team_recv.at[2])
            for part in range(3):
                @pl.when(part < rowm)
                def _():
                    t_copy(part, 0, part).wait_recv()
            x_buf[...] = jnp.zeros_like(x_buf)

            @pl.loop(0, rowm + 1)
            def _(part):
                for side in range(2):
                    x_buf[side] -= dot_n(
                        t_buf[part],
                        a1_buf[pl.ds(4 * part, 4), side].reshape(4 * THIN, WIDE),
                    )
        for to in range(1, 4):
            @pl.when(jnp.logical_and(to > rowm, not start))
            def _():
                t_copy(rowm, to, to).wait_send()
        for side in range(2):
            for part in range(4):
                placed(
                    x_buf.at[side, pl.ds(part * THIN, THIN)],
                    superw.at[col, pl.ds(0, THIN), pl.ds(WIDE, WIDE)],
                    x_recv.at[col], x_send.at[side, part],
                    4 * row4 + part, 2 * rowm + side, True, not start,
                )

    def inverse_ready(at):
        arrived(superw.at[at, pl.ds(0, THIN), pl.ds(WIDE, WIDE)], x_recv.at[at])

    def fill_superw():
        for base, wt in ((0, child_wt), (PAIRS, root_wt)):
            for pair in range(PAIRS):
                superw[base + pair, 0:THIN, 0:WIDE] = wt[2 * pair]
                superw[base + pair, THIN:, WIDE:] = wt[2 * pair + 1]
                superw[base + pair, THIN:, 0:WIDE] = jnp.zeros((THIN, WIDE), jnp.float32)

    def child_trailing(value, block, first):
        for later in range(first, PAIRS):
            acc_f[later] += dot_t(value, pair_rows(child_factor, later, block))

    def lifting(value, block):
        for at in range(PAIRS):
            lift_buf[at] += dot_t(value, pair_rows(coupling, at, block))

    value = None
    for block in range(SINGLES):
        par = block % 2
        pair, side = block // 2, block % 2
        low, high = side * THIN, (side + 1) * THIN

        def col_work():
            if block == 0:
                fill_superw()
            if block == 1:
                to_team(0, child_wt, child_factor)
            if block > 0:
                child_trailing(value, block - 1, pair + 1)
            if block == 3:
                team_first()

        def row_work():
            if block == 1:
                to_team(PAIRS, root_wt, root_factor)
            if block > 0:
                lifting(value, block - 1)
            if block == 3:
                team_second(True)

        total = unpack(over_col(par, pack(acc_f[pair, :, low:high]), col_work))
        pending = child_rhs[pair, :, low:high] - total
        value_now = over_row(par, dot_n(pending, child_wt[block]), row_work)
        value = value_now
        u_ref[pair, :, side * WIDE:(side + 1) * WIDE] = value
        if side == 0:
            acc_f[pair, :, THIN:] += dot_t(value, child_factor[block + 1, block])
        else:
            acc_f[pair + 1] += dot_t(value, pair_rows(child_factor, pair + 1, block))

    for pair in range(SINGLES // 2, PAIRS):
        par = pair % 2

        def col_work():
            if pair == SINGLES // 2:
                child_trailing(value, SINGLES - 1, pair + 1)
                lifting(value, SINGLES - 1)
            else:
                for side in range(2):
                    child_trailing(
                        value[:, side * WIDE:(side + 1) * WIDE], 2 * pair - 2 + side, pair + 1
                    )

        def row_work():
            if pair > SINGLES // 2:
                for side in range(2):
                    lifting(value[:, side * WIDE:(side + 1) * WIDE], 2 * pair - 2 + side)

        pending = child_rhs[pair] - over_col(par, acc_f[pair], col_work)
        inverse_ready(pair)
        value_now = over_row(par, dot_n(pending, superw[pair]), row_work)
        value = value_now
        u_ref[pair] = value
        if pair + 1 < PAIRS:
            for side in range(2):
                acc_f[pair + 1] += dot_t(
                    value[:, side * WIDE:(side + 1) * WIDE],
                    pair_rows(child_factor, pair + 1, 2 * pair + side),
                )

    def lift_copy(at):
        return pltpu.make_async_remote_copy(
            src_ref=lift_buf.at[at, pl.ds(theirs, half)], dst_ref=lift_in.at[at],
            send_sem=lift_send.at[at], recv_sem=lift_recv.at[at],
            device_id=other, device_id_type=MESH,
        )

    for at in range(PAIRS):
        for side in range(2):
            lift_buf[at] += dot_t(
                value[:, side * WIDE:(side + 1) * WIDE],
                pair_rows(coupling, at, 2 * PAIRS - 2 + side),
            )
        lift_copy(at).start()

    def lift_ready(at):
        lift_copy(at).wait_recv()
        acc_r[at] = lift_buf[at, pl.ds(mine, half)] + lift_in[at]
        lift_copy(at).wait_send()

    lift_ready(0)

    def root_forward(pair, carry):
        par = lax.rem(pair, 2)

        def col_work():
            @pl.when(pair == 0)
            def _():
                for at in range(1, PAIRS):
                    lift_ready(at)

            @pl.when(pair > 0)
            def _():
                before = v_ref[jnp.maximum(pair - 1, 0)]

                @pl.loop(pair + 1, PAIRS)
                def _(later):
                    for side in range(2):
                        acc_r[later] += dot_t(
                            before[:, side * WIDE:(side + 1) * WIDE],
                            pair_rows(root_factor, later, 2 * pair - 2 + side),
                        )

        pending = root_rhs[pair, pl.ds(mine, half)] - over_col(par, acc_r[pair], col_work)
        inverse_ready(PAIRS + pair)
        value = over_row(par, dot_n(pending, superw[PAIRS + pair]), lambda: None)
        v_ref[pair] = value

        @pl.when(pair + 1 < PAIRS)
        def _():
            for side in range(2):
                acc_r[pair + 1] += dot_t(
                    value[:, side * WIDE:(side + 1) * WIDE],
                    pair_rows(root_factor, pair + 1, 2 * pair + side),
                )

        return carry

    lax.fori_loop(0, PAIRS, root_forward, 0)

    def s_copy(pair):
        return pltpu.make_async_remote_copy(
            src_ref=s_half.at[pair], dst_ref=s_in.at[pair],
            send_sem=s_send.at[pair], recv_sem=s_recv.at[pair],
            device_id=other, device_id_type=MESH,
        )

    def root_solved(pair):
        s_copy(pair).wait_recv()
        root_out[pair, pl.ds(mine, half)] = s_half[pair]
        root_out[pair, pl.ds(theirs, half)] = s_in[pair]
        s_copy(pair).wait_send()

    def lower(value, pair, earlier):
        for side in range(2):
            acc_c[earlier, :, side * WIDE:(side + 1) * WIDE] += dot_n(
                value, pair_rows(coupling, pair, 2 * earlier + side)
            )

    def root_backward(step, carry):
        par = lax.rem(step, 2)
        pair = PAIRS - 1 - step
        after = jnp.minimum(pair + 1, PAIRS - 1)

        def row_work():
            @pl.when(step > 0)
            def _():
                value = s_half[after]

                @pl.loop(0, pair)
                def _(earlier):
                    for side in range(2):
                        acc_b[earlier, :, side * WIDE:(side + 1) * WIDE] += dot_n(
                            value, pair_rows(root_factor, after, 2 * earlier + side)
                        )

        def col_work():
            @pl.when(step > 0)
            def _():
                root_solved(after)
                value = root_out[after]

                @pl.loop(0, PAIRS)
                def _(earlier):
                    lower(value, after, earlier)

        pending = v_ref[pair] - over_row(par, acc_b[pair], row_work)
        value = over_col(par, dot_t(pending, superw[PAIRS + pair]), col_work)
        s_half[pair] = value
        s_copy(pair).start()

        @pl.when(pair > 0)
        def _():
            before = jnp.maximum(pair - 1, 0)
            for side in range(2):
                acc_b[before, :, side * WIDE:(side + 1) * WIDE] += dot_n(
                    value, pair_rows(root_factor, pair, 2 * before + side)
                )

        return carry

    lax.fori_loop(0, PAIRS, root_backward, 0)
    root_solved(0)
    last = root_out[0]
    lower(last, 0, PAIRS - 1)
    for at in range(SINGLES // 2):
        inverse_ready(at)

    def child_backward(step, carry):
        par = lax.rem(step, 2)
        pair = PAIRS - 1 - step
        after = jnp.minimum(pair + 1, PAIRS - 1)

        def row_work():
            @pl.when(step == 0)
            def _():
                for earlier in range(PAIRS - 1):
                    lower(root_out[0], 0, earlier)

            @pl.when(step > 0)
            def _():
                value = child_out[after]

                @pl.loop(0, pair)
                def _(earlier):
                    for side in range(2):
                        acc_c[earlier, :, side * WIDE:(side + 1) * WIDE] += dot_n(
                            value, pair_rows(child_factor, after, 2 * earlier + side)
                        )

        def col_work():
            @pl.when(step == 0)
            def _():
                to_team(0, child_wt, child_factor, True)

            @pl.when(step == 1)
            def _():
                to_team(PAIRS, root_wt, root_factor, True)
                team_second(False)

        pending = u_ref[pair] - over_row(par, acc_c[pair], row_work)
        value = over_col(par, dot_t(pending, superw[pair]), col_work)
        child_out[pair] = value

        @pl.when(pair > 0)
        def _():
            before = jnp.maximum(pair - 1, 0)
            for side in range(2):
                acc_c[before, :, side * WIDE:(side + 1) * WIDE] += dot_n(
                    value, pair_rows(child_factor, pair, 2 * before + side)
                )

        return carry

    lax.fori_loop(0, PAIRS, child_backward, 0)


def paired(x):
    return jnp.transpose(x.reshape(x.shape[0], PAIRS, 2 * THIN), (1, 0, 2))


def unpaired(x):
    return jnp.transpose(x, (1, 0, 2)).reshape(x.shape[1], 2 * PAIRS, THIN)


def local(root_rhs, child_rhs, root_factor, child_factor, coupling, root_inverse, child_inverse):
    nrhs = root_rhs.shape[0]
    half = nrhs // 2
    vmem = pl.BlockSpec(memory_space=pltpu.VMEM)
    f32 = jnp.float32
    dma = pltpu.SemaphoreType.DMA
    root, child = pl.pallas_call(
        kernel,
        out_shape=(
            jax.ShapeDtypeStruct((PAIRS, nrhs, 2 * THIN), f32),
            jax.ShapeDtypeStruct((PAIRS, nrhs, 2 * THIN), f32),
        ),
        in_specs=[vmem] * 7,
        out_specs=[vmem] * 2,
        scratch_shapes=[
            pltpu.VMEM((PAIRS, nrhs, 2 * WIDE), f32),
            pltpu.VMEM((PAIRS, half, 2 * WIDE), f32),
            pltpu.VMEM((PAIRS, half, 2 * THIN), f32),
            pltpu.VMEM((PAIRS, half, 2 * THIN), f32),
            pltpu.VMEM((PAIRS, nrhs, 2 * THIN), f32),
            pltpu.VMEM((PAIRS, half, 2 * THIN), f32),
            pltpu.VMEM((PAIRS, half, 2 * WIDE), f32),
            pltpu.VMEM((PAIRS, nrhs, 2 * WIDE), f32),
            pltpu.VMEM((2 * PAIRS, 2 * THIN, 2 * WIDE), f32),
            pltpu.VMEM((2, COLS, nrhs, 2 * THIN), f32),
            pltpu.VMEM((2, ROWS, nrhs, 2 * WIDE), f32),
            pltpu.VMEM((PAIRS, nrhs, 2 * THIN), f32),
            pltpu.VMEM((PAIRS, half, 2 * THIN), f32),
            pltpu.VMEM((COLS, 4, THIN, WIDE), f32),
            pltpu.VMEM((COLS, 4, THIN, WIDE), f32),
            pltpu.VMEM((ROWS, 2, THIN, WIDE), f32),
            pltpu.VMEM((4, 4 * THIN, 4 * THIN), f32),
            pltpu.VMEM((2, 4 * THIN, WIDE), f32),
            dma((2, COLS)), dma((2, COLS)), dma((2, ROWS)), dma((2, ROWS)),
            dma((PAIRS,)), dma((PAIRS,)), dma((PAIRS,)), dma((PAIRS,)),
            dma((2 * PAIRS, 12)), dma((3,)), dma((4,)), dma((4,)),
            dma((2, 4)), dma((2 * PAIRS,)),
        ],
        compiler_params=pltpu.CompilerParams(
            collective_id=0, has_side_effects=True, vmem_limit_bytes=48 << 20
        ),
    )(
        paired(root_rhs), paired(child_rhs[0]),
        root_factor, child_factor[0], coupling[0],
        jnp.swapaxes(root_inverse, 1, 2), jnp.swapaxes(child_inverse[0], 1, 2),
    )
    return unpaired(root), unpaired(child)[None]


def solution(mesh):
    in_specs = (
        P(None, None, "row"),
        P("layer", None, None, "row"),
        P(None, None, "row", "col"),
        P("layer", None, None, "row", "col"),
        P("layer", None, None, "row", "col"),
        P(None, "col", "row"),
        P("layer", None, "col", "row"),
    )
    out_specs = (P(None, None, "row"), P("layer", None, None, "row"))
    return jax.shard_map(local, mesh=mesh, in_specs=in_specs, out_specs=out_specs, check_vma=False)
```

time: 830 us -> 333 us (0.40)
  Pallas kernels: 0 us -> 323 us
  blocking collectives: 319 us -> 0 us
  waiting for transfers between devices: 205 us -> 0 us
  starting transfers between devices: 154 us -> 0 us
  matrix products: 61.4 us -> 0 us
  local copies, waits for them, and re-layouts: 54.1 us -> 8.7 us
  other arithmetic: 26.3 us -> 0 us
    pallas_call x0 -> x1, Pallas kernels: none -> 323 us  [local(): pl.pallas_call(kernel, out_shape=(jax.ShapeDtypeStruct((PAIRS, nrhs, 2 *...]
    all_to_all x32 -> x0, blocking collectives: 311 us -> none  [from_everyone(): lax.all_to_all(jnp.broadcast_to(shard[None], (count, *shard.shape)), axis...]
    all_to_all x33 -> x0, waiting for transfers between devices: 205 us -> none  [the longest x32 198 us: from_everyone(): lax.all_to_all(jnp.broadcast_to(shard[None], (count, *shard.shape)), axis...]
    all_to_all x33 -> x0, starting transfers between devices: 154 us -> none  [the longest x32 149 us: from_everyone(): lax.all_to_all(jnp.broadcast_to(shard[None], (count, *shard.shape)), axis...]
    dot_general x66 -> x0, matrix products: 61.4 us -> none  [the longest x16 20.2 us: forward_step(): jnp.einsum('jna,jba->nb', solved, row_tiles, precision=precise)]
    all_to_all x33 -> x0, other arithmetic: 25.1 us -> none  [the longest x32 24.3 us: from_everyone(): lax.all_to_all(jnp.broadcast_to(shard[None], (count, *shard.shape)), axis...]
    while x65 -> x0, local copies, waits for them, and re-layouts: 16.9 us -> none
    all_to_all x33 -> x0, local copies, waits for them, and re-layouts: 16.9 us -> none  [the longest x32 16.4 us: from_everyone(): lax.all_to_all(jnp.broadcast_to(shard[None], (count, *shard.shape)), axis...]
  transfers between devices with their start and end apart: 33 -> 0, of which waited for: 33 -> 0; matrix products, arithmetic and copies ran while one was open for 0% -> 0% of each run, Pallas kernels for 0% -> 0%
where the time goes in v2:
time: 333 us; the launch traced here: 332 us
  Pallas kernels  323 us (97%)
  local copies, waits for them, and re-layouts  8.7 us (3%)
    pallas_call x1, Pallas kernels, local(): pl.pallas_call(kernel, out_shape=(jax.ShapeDtypeStruct((PAIRS, nrhs, 2 *...  323 us

profile of v2, /device:TPU:1, one launch (start us, length us, event | category | flops | bytes accessed | tf_op | source)
XLA Modules:
  0.0 332.3 jit_solution(5975361468111794400)
XLA Ops:
  0.6 1.0 reshape.10
  1.6 1.0 reshape_squeeze.3
  2.7 0.0 copy-start
  2.7 1.6 copy-done
  4.2 0.0 copy-start.1
  4.3 1.6 copy-done.1
  5.8 0.0 copy-start.2
  5.8 0.9 copy-done.2
  6.8 0.0 copy-start.3
  6.8 0.9 copy-done.3
  7.7 323.0 %shard_map.86 = (f32[4,32,128]{2,1,0:T(8,128)S(1)}, f32[4,32,128]{2,1,0:T(8,128)S(1)}) custom-call(f32[4,32,128]{2,1,0:T(8,128)S(1)} %get-tuple-element.7.root_rhs, f32[4,32,128]{2,1,0:T(8,128)S(1)} %get-tuple-element.6.child_rhs, f32[8,8,64,128]{3,2,1,0:T(8,128)S(1)} %copy-done, f32[8,8,64,128]{3,2,1,0:T(8,128)S(1)} %bitcast.14, ...), custom_call_target="tpu_custom_call" | custom-call | tf_op jit(solution)/shard_map/pallas_call | solution.py:493
  330.8 0.8 broadcast_in_dim_reshape.3
  331.6 0.8 reshape.11
  (3 shorter events, 0.1 us)
Async XLA Ops:
  2.7 1.6 copy-start
  4.2 1.6 copy-start.1
  5.8 0.9 copy-start.2
  6.8 0.9 copy-start.3

commit v3 on v2

--- a/solution.py
+++ b/solution.py
@@ -43,12 +43,13 @@
 
 
 def kernel(
-    root_rhs, child_rhs, root_factor, child_factor, coupling, root_wt, child_wt,
+    root_rhs, child_rhs, root_factor_hbm, child_factor_hbm, coupling_hbm, root_wt_hbm, child_wt_hbm,
     root_out, child_out,
+    root_factor, child_factor, coupling, root_wt, child_wt,
     u_ref, v_ref, s_half, s_in, acc_f, acc_r, acc_b, acc_c, superw,
     col_buf, row_buf, lift_buf, lift_in, a0_buf, c_buf, a1_buf, t_buf, x_buf,
     col_send, col_recv, row_send, row_recv, lift_send, lift_recv, s_send, s_recv,
-    team_send, team_recv, t_send, t_recv, x_send, x_recv,
+    team_send, team_recv, t_send, t_recv, x_send, x_recv, in_sem,
 ):
     layer = lax.axis_index("layer")
     row = lax.axis_index("row")
@@ -63,6 +64,15 @@
     mine = pl.multiple_of(layer * half, half)
     theirs = pl.multiple_of((1 - layer) * half, half)
 
+    loads = [
+        pltpu.make_async_copy(src, dst, in_sem.at[at])
+        for at, (src, dst) in enumerate((
+            (child_wt_hbm, child_wt), (child_factor_hbm, child_factor),
+            (coupling_hbm, coupling), (root_wt_hbm, root_wt), (root_factor_hbm, root_factor),
+        ))
+    ]
+    for load in loads:
+        load.start()
     barrier = pltpu.get_barrier_semaphore()
     for peer in col_peers:
         pl.semaphore_signal(barrier, inc=1, device_id=(layer, row, peer), device_id_type=MESH)
@@ -119,14 +129,22 @@
             row_copy(par, row, at, height, width, peer).wait_send()
         return total
 
-    def placed(src, dst, recv, send, to_row, to_col, wanted, finish):
-        here = jnp.logical_and(to_row == row, to_col == col)
+    phases = (
+        (0, 2, child_wt, child_factor, 2),
+        (2, 2 * layer, root_wt, root_factor, PAIRS + 2 * layer),
+        (1, 0, child_wt, child_factor, 0),
+    )
+
+    def placed(src, dst, recv, send, to_layer, to_row, to_col, wanted, finish):
+        here = jnp.logical_and(
+            to_layer == layer, jnp.logical_and(to_row == row, to_col == col)
+        )
 
         @pl.when(jnp.logical_and(wanted, jnp.logical_not(here)))
         def _():
             copy = pltpu.make_async_remote_copy(
                 src_ref=src, dst_ref=dst, send_sem=send, recv_sem=recv,
-                device_id=(layer, to_row, to_col), device_id_type=MESH,
+                device_id=(to_layer, to_row, to_col), device_id_type=MESH,
             )
             copy.wait_send() if finish else copy.start()
 
@@ -135,26 +153,28 @@
             def _():
                 pltpu.make_async_copy(src, dst, recv).start()
 
-    def to_team(base, wt, factor, finish=False):
-        @pl.loop(0, PAIRS)
-        def _(turn):
-            pair = lax.rem(turn + col, PAIRS)
-            team = base + pair
-            for j in range(4):
-                placed(
-                    wt.at[2 * pair], a0_buf.at[col, rowm], team_recv.at[0],
-                    team_send.at[team, j], 4 * row4 + j, team, col2 >= row4, finish,
-                )
-            for i in range(4):
-                placed(
-                    factor.at[2 * pair + 1, 2 * pair], c_buf.at[col, rowm], team_recv.at[1],
-                    team_send.at[team, 4 + i], 4 * i + row4, team, col2 >= i, finish,
-                )
-            for i in range(4):
-                placed(
-                    wt.at[2 * pair + 1], a1_buf.at[row, colm], team_recv.at[2],
-                    team_send.at[team, 8 + i], 4 * i + col2, team, row4 <= col2, finish,
-                )
+    def to_team(phase, kind, finish=False):
+        base, first, wt, factor, _ = phases[phase]
+        for which in range(2):
+            pair, team = first + which, base + 4 * which
+            for at in range(4):
+                send = team_send.at[phase, which, 4 * kind + at]
+                if kind == 0:
+                    placed(
+                        wt.at[2 * pair], a0_buf.at[col, rowm], team_recv.at[0], send,
+                        layer, 4 * row4 + at, team, col2 >= row4, finish,
+                    )
+                elif kind == 1:
+                    placed(
+                        factor.at[2 * pair + 1, 2 * pair], c_buf.at[col, rowm],
+                        team_recv.at[1], send,
+                        layer, 4 * at + row4, team, col2 >= at, finish,
+                    )
+                else:
+                    placed(
+                        wt.at[2 * pair + 1], a1_buf.at[row, colm], team_recv.at[2], send,
+                        layer, 4 * at + col2, team, row4 <= col2, finish,
+                    )
 
     def arrived(ref, sem):
         pltpu.make_async_copy(ref, ref, sem).wait()
@@ -166,7 +186,13 @@
             device_id=(layer, 4 * row4 + to, col), device_id_type=MESH,
         )
 
-    def team_first():
+    def team_first(phase):
+        pl.when(lax.rem(col, 4) == phases[phase][0])(team_product)
+
+    def team_second(phase, start=True):
+        pl.when(lax.rem(col, 4) == phases[phase][0])(lambda: team_result(phase, start))
+
+    def team_product():
         for part in range(4):
             @pl.when(row4 == part)
             def _():
@@ -185,7 +211,7 @@
             def _():
                 t_copy(rowm, to, to).start()
 
-    def team_second(start):
+    def team_result(phase, start):
         if start:
             for part in range(4):
                 @pl.when(rowm == part)
@@ -204,18 +230,24 @@
                         t_buf[part],
                         a1_buf[pl.ds(4 * part, 4), side].reshape(4 * THIN, WIDE),
                     )
-        for to in range(1, 4):
-            @pl.when(jnp.logical_and(to > rowm, not start))
-            def _():
-                t_copy(rowm, to, to).wait_send()
-        for side in range(2):
-            for part in range(4):
-                placed(
-                    x_buf.at[side, pl.ds(part * THIN, THIN)],
-                    superw.at[col, pl.ds(0, THIN), pl.ds(WIDE, WIDE)],
-                    x_recv.at[col], x_send.at[side, part],
-                    4 * row4 + part, 2 * rowm + side, True, not start,
-                )
+        else:
+            for to in range(1, 4):
+                @pl.when(to > rowm)
+                def _():
+                    t_copy(rowm, to, to).wait_send()
+        slot = phases[phase][4] + col // 4
+        for to in range(2):
+            if phase != 1 and to == 1:
+                continue
+            for side in range(2):
+                for part in range(4):
+                    placed(
+                        x_buf.at[side, pl.ds(part * THIN, THIN)],
+                        superw.at[slot, pl.ds(0, THIN), pl.ds(WIDE, WIDE)],
+                        x_recv.at[slot], x_send.at[to, side, part],
+                        layer if to == 0 else 1 - layer,
+                        4 * row4 + part, 2 * rowm + side, True, not start,
+                    )
 
     def inverse_ready(at):
         arrived(superw.at[at, pl.ds(0, THIN), pl.ds(WIDE, WIDE)], x_recv.at[at])
@@ -242,25 +274,34 @@
         low, high = side * THIN, (side + 1) * THIN
 
         def col_work():
+            child_trailing(value, block - 1, pair + 1)
+            if block == 1:
+                to_team(0, 0)
+            if block == 2:
+                to_team(0, 2)
+            if block == 3:
+                team_first(0)
+
+        def row_work():
             if block == 0:
+                loads[1].wait()
+                loads[2].wait()
+                loads[3].wait()
+                loads[4].wait()
                 fill_superw()
+            else:
+                lifting(value, block - 1)
             if block == 1:
-                to_team(0, child_wt, child_factor)
-            if block > 0:
-                child_trailing(value, block - 1, pair + 1)
+                to_team(0, 1)
             if block == 3:
-                team_first()
-
-        def row_work():
-            if block == 1:
-                to_team(PAIRS, root_wt, root_factor)
-            if block > 0:
-                lifting(value, block - 1)
-            if block == 3:
-                team_second(True)
-
-        total = unpack(over_col(par, pack(acc_f[pair, :, low:high]), col_work))
-        pending = child_rhs[pair, :, low:high] - total
+                team_second(0)
+                to_team(1, 0)
+
+        pending = child_rhs[pair, :, low:high]
+        if block == 0:
+            loads[0].wait()
+        else:
+            pending = pending - unpack(over_col(par, pack(acc_f[pair, :, low:high]), col_work))
         value_now = over_row(par, dot_n(pending, child_wt[block]), row_work)
         value = value_now
         u_ref[pair, :, side * WIDE:(side + 1) * WIDE] = value
@@ -274,6 +315,7 @@
 
         def col_work():
             if pair == SINGLES // 2:
+                to_team(1, 1)
                 child_trailing(value, SINGLES - 1, pair + 1)
                 lifting(value, SINGLES - 1)
             else:
@@ -281,11 +323,15 @@
                     child_trailing(
                         value[:, side * WIDE:(side + 1) * WIDE], 2 * pair - 2 + side, pair + 1
                     )
+                team_first(1)
 
         def row_work():
-            if pair > SINGLES // 2:
+            if pair == SINGLES // 2:
+                to_team(1, 2)
+            else:
                 for side in range(2):
                     lifting(value[:, side * WIDE:(side + 1) * WIDE], 2 * pair - 2 + side)
+                team_second(1)
 
         pending = child_rhs[pair] - over_col(par, acc_f[pair], col_work)
         inverse_ready(pair)
@@ -344,7 +390,12 @@
 
         pending = root_rhs[pair, pl.ds(mine, half)] - over_col(par, acc_r[pair], col_work)
         inverse_ready(PAIRS + pair)
-        value = over_row(par, dot_n(pending, superw[PAIRS + pair]), lambda: None)
+
+        def row_work():
+            for kind in range(3):
+                pl.when(pair == kind)(lambda: to_team(2, kind))
+
+        value = over_row(par, dot_n(pending, superw[PAIRS + pair]), row_work)
         v_ref[pair] = value
 
         @pl.when(pair + 1 < PAIRS)
@@ -378,34 +429,37 @@
                 value, pair_rows(coupling, pair, 2 * earlier + side)
             )
 
-    def root_backward(step, carry):
+    def root_backward(step, first):
         par = lax.rem(step, 2)
         pair = PAIRS - 1 - step
         after = jnp.minimum(pair + 1, PAIRS - 1)
 
         def row_work():
-            @pl.when(step > 0)
-            def _():
-                value = s_half[after]
-
-                @pl.loop(0, pair)
-                def _(earlier):
-                    for side in range(2):
-                        acc_b[earlier, :, side * WIDE:(side + 1) * WIDE] += dot_n(
-                            value, pair_rows(root_factor, after, 2 * earlier + side)
-                        )
+            value = s_half[after]
+
+            @pl.loop(0, pair)
+            def _(earlier):
+                for side in range(2):
+                    acc_b[earlier, :, side * WIDE:(side + 1) * WIDE] += dot_n(
+                        value, pair_rows(root_factor, after, 2 * earlier + side)
+                    )
 
         def col_work():
-            @pl.when(step > 0)
-            def _():
-                root_solved(after)
-                value = root_out[after]
-
-                @pl.loop(0, PAIRS)
-                def _(earlier):
-                    lower(value, after, earlier)
-
-        pending = v_ref[pair] - over_row(par, acc_b[pair], row_work)
+            if first:
+                team_first(2)
+                return
+            root_solved(after)
+            value = root_out[after]
+
+            @pl.loop(0, PAIRS)
+            def _(earlier):
+                lower(value, after, earlier)
+
+            pl.when(step == 1)(lambda: team_second(2))
+
+        pending = v_ref[pair]
+        if not first:
+            pending = pending - over_row(1 - par, acc_b[pair], row_work)
         value = over_col(par, dot_t(pending, superw[PAIRS + pair]), col_work)
         s_half[pair] = value
         s_copy(pair).start()
@@ -418,9 +472,10 @@
                     value, pair_rows(root_factor, pair, 2 * before + side)
                 )
 
-        return carry
-
-    lax.fori_loop(0, PAIRS, root_backward, 0)
+        return 0
+
+    root_backward(jnp.int32(0), True)
+    lax.fori_loop(1, PAIRS, lambda step, carry: root_backward(step, False), 0)
     root_solved(0)
     last = root_out[0]
     lower(last, 0, PAIRS - 1)
@@ -450,16 +505,14 @@
                         )
 
         def col_work():
-            @pl.when(step == 0)
-            def _():
-                to_team(0, child_wt, child_factor, True)
-
-            @pl.when(step == 1)
-            def _():
-                to_team(PAIRS, root_wt, root_factor, True)
-                team_second(False)
-
-        pending = u_ref[pair] - over_row(par, acc_c[pair], row_work)
+            for phase in range(3):
+                @pl.when(step == phase)
+                def _():
+                    for kind in range(3):
+                        to_team(phase, kind, True)
+                    team_second(phase, False)
+
+        pending = u_ref[pair] - over_row(1 - par, acc_c[pair], row_work)
         value = over_col(par, dot_t(pending, superw[pair]), col_work)
         child_out[pair] = value
 
@@ -496,9 +549,14 @@
             jax.ShapeDtypeStruct((PAIRS, nrhs, 2 * THIN), f32),
             jax.ShapeDtypeStruct((PAIRS, nrhs, 2 * THIN), f32),
         ),
-        in_specs=[vmem] * 7,
+        in_specs=[vmem] * 2 + [pl.BlockSpec(memory_space=pltpu.HBM)] * 5,
         out_specs=[vmem] * 2,
         scratch_shapes=[
+            pltpu.VMEM(root_factor.shape, f32),
+            pltpu.VMEM(root_factor.shape, f32),
+            pltpu.VMEM(root_factor.shape, f32),
+            pltpu.VMEM((2 * PAIRS, THIN, WIDE), f32),
+            pltpu.VMEM((2 * PAIRS, THIN, WIDE), f32),
             pltpu.VMEM((PAIRS, nrhs, 2 * WIDE), f32),
             pltpu.VMEM((PAIRS, half, 2 * WIDE), f32),
             pltpu.VMEM((PAIRS, half, 2 * THIN), f32),
@@ -519,8 +577,8 @@
             pltpu.VMEM((2, 4 * THIN, WIDE), f32),
             dma((2, COLS)), dma((2, COLS)), dma((2, ROWS)), dma((2, ROWS)),
             dma((PAIRS,)), dma((PAIRS,)), dma((PAIRS,)), dma((PAIRS,)),
-            dma((2 * PAIRS, 12)), dma((3,)), dma((4,)), dma((4,)),
-            dma((2, 4)), dma((2 * PAIRS,)),
+            dma((3, 2, 12)), dma((3,)), dma((4,)), dma((4,)),
+            dma((2, 2, 4)), dma((2 * PAIRS,)), dma((5,)),
         ],
         compiler_params=pltpu.CompilerParams(
             collective_id=0, has_side_effects=True, vmem_limit_bytes=48 << 20

time: 333 us -> 298 us (0.89)
  Pallas kernels: 323 us -> 288 us
    pallas_call x1, Pallas kernels: 323 us -> 288 us  [local(): pl.pallas_call(kernel, out_shape=(jax.ShapeDtypeStruct((PAIRS, nrhs, 2 *...]
where the time goes in v3:
time: 298 us
  Pallas kernels  288 us (97%)
  local copies, waits for them, and re-layouts  8.7 us (3%)
    pallas_call x1, Pallas kernels, local(): pl.pallas_call(kernel, out_shape=(jax.ShapeDtypeStruct((PAIRS, nrhs, 2 *...  288 us

profile of v3, /device:TPU:1, one launch (start us, length us, event | category | flops | bytes accessed | tf_op | source)
XLA Modules:
  0.0 297.7 jit_solution(13006602071408908198)
XLA Ops:
  0.6 1.0 reshape.10
  1.6 1.0 reshape_squeeze.3
  2.7 0.0 copy-start
  2.7 1.6 copy-done
  4.2 0.0 copy-start.1
  4.3 1.6 copy-done.1
  5.8 0.0 copy-start.2
  5.8 0.9 copy-done.2
  6.8 0.0 copy-start.3
  6.8 0.9 copy-done.3
  7.7 288.4 %shard_map.86 = (f32[4,32,128]{2,1,0:T(8,128)S(1)}, f32[4,32,128]{2,1,0:T(8,128)S(1)}) custom-call(f32[4,32,128]{2,1,0:T(8,128)S(1)} %get-tuple-element.7.root_rhs, f32[4,32,128]{2,1,0:T(8,128)S(1)} %get-tuple-element.6.child_rhs, f32[8,8,64,128]{3,2,1,0:T(8,128)S(1)} %copy-done, f32[8,8,64,128]{3,2,1,0:T(8,128)S(1)} %bitcast.14, ...), custom_call_target="tpu_custom_call" | custom-call | tf_op jit(solution)/shard_map/pallas_call | solution.py:546
  296.2 0.8 broadcast_in_dim_reshape.3
  297.0 0.8 reshape.11
  (3 shorter events, 0.1 us)
Async XLA Ops:
  2.7 1.6 copy-start
  4.2 1.6 copy-start.1
  5.8 0.9 copy-start.2
  6.8 0.9 copy-start.3

commit v4 on v3

--- a/solution.py
+++ b/solution.py
@@ -47,9 +47,9 @@
     root_out, child_out,
     root_factor, child_factor, coupling, root_wt, child_wt,
     u_ref, v_ref, s_half, s_in, acc_f, acc_r, acc_b, acc_c, superw,
-    col_buf, row_buf, lift_buf, lift_in, a0_buf, c_buf, a1_buf, t_buf, x_buf,
+    col_buf, row_buf, lift_buf, lift_in, a0_buf, c_buf, a1_buf, t_buf, x_out, x_in, x_buf,
     col_send, col_recv, row_send, row_recv, lift_send, lift_recv, s_send, s_recv,
-    team_send, team_recv, t_send, t_recv, x_send, x_recv, in_sem,
+    z_send, z_recv, xy_send, xy_recv, x_send, x_recv, in_sem,
 ):
     layer = lax.axis_index("layer")
     row = lax.axis_index("row")
@@ -153,88 +153,134 @@
             def _():
                 pltpu.make_async_copy(src, dst, recv).start()
 
-    def to_team(phase, kind, finish=False):
+    def arrived(ref, sem):
+        pltpu.make_async_copy(ref, ref, sem).wait()
+
+    def gather_z(phase, finish=False):
         base, first, wt, factor, _ = phases[phase]
         for which in range(2):
             pair, team = first + which, base + 4 * which
-            for at in range(4):
-                send = team_send.at[phase, which, 4 * kind + at]
-                if kind == 0:
-                    placed(
-                        wt.at[2 * pair], a0_buf.at[col, rowm], team_recv.at[0], send,
-                        layer, 4 * row4 + at, team, col2 >= row4, finish,
-                    )
-                elif kind == 1:
-                    placed(
-                        factor.at[2 * pair + 1, 2 * pair], c_buf.at[col, rowm],
-                        team_recv.at[1], send,
-                        layer, 4 * at + row4, team, col2 >= at, finish,
-                    )
-                else:
-                    placed(
-                        wt.at[2 * pair + 1], a1_buf.at[row, colm], team_recv.at[2], send,
-                        layer, 4 * at + col2, team, row4 <= col2, finish,
-                    )
-
-    def arrived(ref, sem):
-        pltpu.make_async_copy(ref, ref, sem).wait()
-
-    def t_copy(slot, at, to):
+            needed = col2 >= row4
+            for kind, (src, dst, wanted) in enumerate((
+                (wt.at[2 * pair], a0_buf.at[rowm, col], needed),
+                (factor.at[2 * pair + 1, 2 * pair], c_buf.at[row4, col], True),
+                (wt.at[2 * pair + 1], a1_buf.at[row4, col], needed),
+            )):
+                placed(
+                    src, dst, z_recv.at[kind], z_send.at[phase, which, kind],
+                    layer, row, team, wanted, finish,
+                )
+
+    def team_copy(src, dst, send, recv, to_row):
         return pltpu.make_async_remote_copy(
-            src_ref=t_buf.at[slot], dst_ref=t_buf.at[slot],
-            send_sem=t_send.at[at], recv_sem=t_recv.at[slot],
-            device_id=(layer, 4 * row4 + to, col), device_id_type=MESH,
+            src_ref=src, dst_ref=dst, send_sem=send, recv_sem=recv,
+            device_id=(layer, to_row, col), device_id_type=MESH,
         )
 
-    def team_first(phase):
-        pl.when(lax.rem(col, 4) == phases[phase][0])(team_product)
-
-    def team_second(phase, start=True):
-        pl.when(lax.rem(col, 4) == phases[phase][0])(lambda: team_result(phase, start))
-
-    def team_product():
+    def tail(ref, slot, part):
+        return ref.at[slot, pl.ds(2 * part, COLS - 2 * part)]
+
+    def a0_copy(part, slot, to):
+        where = tail(a0_buf, slot, part)
+        return team_copy(where, where, xy_send.at[0, to], xy_recv.at[0, slot], 4 * row4 + to)
+
+    def c_copy(part, slot, to):
+        where = tail(c_buf, slot, part)
+        return team_copy(where, where, xy_send.at[1, to], xy_recv.at[1, slot], 4 * to + rowm)
+
+    def a1_copy(part, slot, to):
+        where = tail(a1_buf, slot, part)
+        return team_copy(where, where, xy_send.at[2, to], xy_recv.at[2, slot], 4 * to + rowm)
+
+    def part_copy(slot, to):
+        return team_copy(
+            x_out.at[pl.ds(2 * to, 2)], x_in.at[slot],
+            xy_send.at[3, to], xy_recv.at[3, slot], 4 * row4 + to,
+        )
+
+    def in_team(phase, work):
+        pl.when(lax.rem(col, 4) == phases[phase][0])(work)
+
+    def gather_xy():
+        arrived(c_buf.at[row4], z_recv.at[1])
+        for to in range(4):
+            @pl.when(row4 != to)
+            def _():
+                c_copy(to, row4, to).start()
         for part in range(4):
             @pl.when(row4 == part)
             def _():
-                arrived(a0_buf.at[pl.ds(2 * part, COLS - 2 * part)], team_recv.at[0])
-                arrived(c_buf.at[pl.ds(2 * part, COLS - 2 * part)], team_recv.at[1])
-        t_buf[rowm] = jnp.zeros((4 * THIN, 4 * THIN), jnp.float32)
+                arrived(tail(a0_buf, rowm, part), z_recv.at[0])
+                for to in range(4):
+                    @pl.when(rowm != to)
+                    def _():
+                        a0_copy(part, rowm, to).start()
+                arrived(tail(a1_buf, row4, part), z_recv.at[2])
+                for to in range(4):
+                    if to != part:
+                        a1_copy(part, row4, to).start()
+
+    def first_product():
+        for part in range(4):
+            @pl.when(row4 == part)
+            def _():
+                for slot in range(4):
+                    @pl.when(rowm != slot)
+                    def _():
+                        a0_copy(part, slot, slot).wait_recv()
+                    if slot != part:
+                        c_copy(part, slot, slot).wait_recv()
+        t_buf[...] = jnp.zeros_like(t_buf)
 
         @pl.loop(2 * row4, COLS)
         def _(at):
-            t_buf[rowm] += dot_t(
-                a0_buf[at].reshape(4 * THIN, WIDE), c_buf[at].reshape(4 * THIN, WIDE)
+            t_buf[...] += dot_t(
+                a0_buf[:, at].reshape(4 * THIN, WIDE), c_buf[:, at].reshape(4 * THIN, WIDE)
             )
 
-        for to in range(1, 4):
-            @pl.when(to > rowm)
-            def _():
-                t_copy(rowm, to, to).start()
-
-    def team_result(phase, start):
-        if start:
+    def second_product():
+        for slot in range(4):
+            @pl.when(row4 != slot)
+            def _():
+                a1_copy(slot, slot, slot).wait_recv()
+        for at in range(COLS):
+            deep = at // 2 + 1
+            x_out[at] = dot_n(
+                t_buf[:, 0:deep * THIN], a1_buf[0:deep, at].reshape(deep * THIN, WIDE)
+            )
+            if at % 2 == 1:
+                @pl.when(rowm != at // 2)
+                def _():
+                    part_copy(rowm, at // 2).start()
+
+    def spread(phase, finish=False):
+        if finish:
             for part in range(4):
-                @pl.when(rowm == part)
+                @pl.when(row4 == part)
                 def _():
-                    arrived(a1_buf.at[pl.ds(0, 4 * part + 4)], team_recv.at[2])
-            for part in range(3):
-                @pl.when(part < rowm)
+                    for to in range(4):
+                        @pl.when(rowm != to)
+                        def _():
+                            a0_copy(part, rowm, to).wait_send()
+                        if to != part:
+                            a1_copy(part, row4, to).wait_send()
+            for to in range(4):
+                @pl.when(row4 != to)
                 def _():
-                    t_copy(part, 0, part).wait_recv()
-            x_buf[...] = jnp.zeros_like(x_buf)
-
-            @pl.loop(0, rowm + 1)
-            def _(part):
-                for side in range(2):
-                    x_buf[side] -= dot_n(
-                        t_buf[part],
-                        a1_buf[pl.ds(4 * part, 4), side].reshape(4 * THIN, WIDE),
-                    )
+                    c_copy(to, row4, to).wait_send()
+                @pl.when(rowm != to)
+                def _():
+                    part_copy(rowm, to).wait_send()
         else:
-            for to in range(1, 4):
-                @pl.when(to > rowm)
+            x_in[rowm] = x_out[pl.ds(2 * rowm, 2)]
+            for slot in range(4):
+                @pl.when(rowm != slot)
                 def _():
-                    t_copy(rowm, to, to).wait_send()
+                    part_copy(slot, slot).wait_recv()
+            for side in range(2):
+                x_buf[side] = -(
+                    (x_in[0, side] + x_in[1, side]) + (x_in[2, side] + x_in[3, side])
+                )
         slot = phases[phase][4] + col // 4
         for to in range(2):
             if phase != 1 and to == 1:
@@ -246,7 +292,7 @@
                         superw.at[slot, pl.ds(0, THIN), pl.ds(WIDE, WIDE)],
                         x_recv.at[slot], x_send.at[to, side, part],
                         layer if to == 0 else 1 - layer,
-                        4 * row4 + part, 2 * rowm + side, True, not start,
+                        4 * row4 + part, 2 * rowm + side, True, finish,
                     )
 
     def inverse_ready(at):
@@ -274,13 +320,13 @@
         low, high = side * THIN, (side + 1) * THIN
 
         def col_work():
+            if block == 1:
+                gather_z(0)
+            if block == 2:
+                in_team(0, gather_xy)
+            if block == 3:
+                in_team(0, second_product)
             child_trailing(value, block - 1, pair + 1)
-            if block == 1:
-                to_team(0, 0)
-            if block == 2:
-                to_team(0, 2)
-            if block == 3:
-                team_first(0)
 
         def row_work():
             if block == 0:
@@ -291,11 +337,11 @@
                 fill_superw()
             else:
                 lifting(value, block - 1)
-            if block == 1:
-                to_team(0, 1)
+            if block == 2:
+                in_team(0, first_product)
             if block == 3:
-                team_second(0)
-                to_team(1, 0)
+                in_team(0, lambda: spread(0))
+                gather_z(1)
 
         pending = child_rhs[pair, :, low:high]
         if block == 0:
@@ -315,7 +361,7 @@
 
         def col_work():
             if pair == SINGLES // 2:
-                to_team(1, 1)
+                in_team(1, gather_xy)
                 child_trailing(value, SINGLES - 1, pair + 1)
                 lifting(value, SINGLES - 1)
             else:
@@ -323,15 +369,15 @@
                     child_trailing(
                         value[:, side * WIDE:(side + 1) * WIDE], 2 * pair - 2 + side, pair + 1
                     )
-                team_first(1)
+                in_team(1, second_product)
 
         def row_work():
             if pair == SINGLES // 2:
-                to_team(1, 2)
+                in_team(1, first_product)
             else:
                 for side in range(2):
                     lifting(value[:, side * WIDE:(side + 1) * WIDE], 2 * pair - 2 + side)
-                team_second(1)
+                in_team(1, lambda: spread(1))
 
         pending = child_rhs[pair] - over_col(par, acc_f[pair], col_work)
         inverse_ready(pair)
@@ -392,8 +438,10 @@
         inverse_ready(PAIRS + pair)
 
         def row_work():
-            for kind in range(3):
-                pl.when(pair == kind)(lambda: to_team(2, kind))
+            pl.when(pair == 0)(lambda: gather_z(2))
+            pl.when(pair == 1)(lambda: in_team(2, gather_xy))
+            pl.when(pair == 2)(lambda: in_team(2, first_product))
+            pl.when(pair == 3)(lambda: in_team(2, second_product))
 
         value = over_row(par, dot_n(pending, superw[PAIRS + pair]), row_work)
         v_ref[pair] = value
@@ -446,7 +494,7 @@
 
         def col_work():
             if first:
-                team_first(2)
+                in_team(2, lambda: spread(2))
                 return
             root_solved(after)
             value = root_out[after]
@@ -454,8 +502,6 @@
             @pl.loop(0, PAIRS)
             def _(earlier):
                 lower(value, after, earlier)
-
-            pl.when(step == 1)(lambda: team_second(2))
 
         pending = v_ref[pair]
         if not first:
@@ -508,9 +554,8 @@
             for phase in range(3):
                 @pl.when(step == phase)
                 def _():
-                    for kind in range(3):
-                        to_team(phase, kind, True)
-                    team_second(phase, False)
+                    gather_z(phase, True)
+                    in_team(phase, lambda: spread(phase, True))
 
         pending = u_ref[pair] - over_row(1 - par, acc_c[pair], row_work)
         value = over_col(par, dot_t(pending, superw[pair]), col_work)
@@ -570,14 +615,16 @@
             pltpu.VMEM((2, ROWS, nrhs, 2 * WIDE), f32),
             pltpu.VMEM((PAIRS, nrhs, 2 * THIN), f32),
             pltpu.VMEM((PAIRS, half, 2 * THIN), f32),
-            pltpu.VMEM((COLS, 4, THIN, WIDE), f32),
-            pltpu.VMEM((COLS, 4, THIN, WIDE), f32),
-            pltpu.VMEM((ROWS, 2, THIN, WIDE), f32),
-            pltpu.VMEM((4, 4 * THIN, 4 * THIN), f32),
+            pltpu.VMEM((4, COLS, THIN, WIDE), f32),
+            pltpu.VMEM((4, COLS, THIN, WIDE), f32),
+            pltpu.VMEM((4, COLS, THIN, WIDE), f32),
+            pltpu.VMEM((4 * THIN, 4 * THIN), f32),
+            pltpu.VMEM((COLS, 4 * THIN, WIDE), f32),
+            pltpu.VMEM((4, 2, 4 * THIN, WIDE), f32),
             pltpu.VMEM((2, 4 * THIN, WIDE), f32),
             dma((2, COLS)), dma((2, COLS)), dma((2, ROWS)), dma((2, ROWS)),
             dma((PAIRS,)), dma((PAIRS,)), dma((PAIRS,)), dma((PAIRS,)),
-            dma((3, 2, 12)), dma((3,)), dma((4,)), dma((4,)),
+            dma((3, 2, 3)), dma((3,)), dma((4, 4)), dma((4, 4)),
             dma((2, 2, 4)), dma((2 * PAIRS,)), dma((5,)),
         ],
         compiler_params=pltpu.CompilerParams(

time: 298 us -> 256 us (0.86)
  Pallas kernels: 288 us -> 246 us
    pallas_call x1, Pallas kernels: 288 us -> 246 us  [local(): pl.pallas_call(kernel, out_shape=(jax.ShapeDtypeStruct((PAIRS, nrhs, 2 *...]
where the time goes in v4:
time: 256 us
  Pallas kernels  246 us (96%)
  local copies, waits for them, and re-layouts  8.7 us (3%)
    pallas_call x1, Pallas kernels, local(): pl.pallas_call(kernel, out_shape=(jax.ShapeDtypeStruct((PAIRS, nrhs, 2 *...  246 us

profile of v4, /device:TPU:1, one launch (start us, length us, event | category | flops | bytes accessed | tf_op | source)
XLA Modules:
  0.0 255.5 jit_solution(6869922395655187793)
XLA Ops:
  0.6 1.0 reshape.10
  1.6 1.0 reshape_squeeze.3
  2.7 0.0 copy-start
  2.7 1.6 copy-done
  4.2 0.0 copy-start.1
  4.3 1.6 copy-done.1
  5.8 0.0 copy-start.2
  5.8 0.9 copy-done.2
  6.8 0.0 copy-start.3
  6.8 0.9 copy-done.3
  7.7 246.1 %shard_map.86 = (f32[4,32,128]{2,1,0:T(8,128)S(1)}, f32[4,32,128]{2,1,0:T(8,128)S(1)}) custom-call(f32[4,32,128]{2,1,0:T(8,128)S(1)} %get-tuple-element.7.root_rhs, f32[4,32,128]{2,1,0:T(8,128)S(1)} %get-tuple-element.6.child_rhs, f32[8,8,64,128]{3,2,1,0:T(8,128)S(1)} %copy-done, f32[8,8,64,128]{3,2,1,0:T(8,128)S(1)} %bitcast.14, ...), custom_call_target="tpu_custom_call" | custom-call | tf_op jit(solution)/shard_map/pallas_call | solution.py:591
  254.0 0.8 broadcast_in_dim_reshape.3
  254.8 0.8 reshape.11
  (3 shorter events, 0.1 us)
Async XLA Ops:
  2.7 1.6 copy-start
  4.2 1.6 copy-start.1
  5.8 0.9 copy-start.2
  6.8 0.9 copy-start.3

commit v5 on v4

--- a/solution.py
+++ b/solution.py
@@ -12,6 +12,7 @@
 THIN = 64
 WIDE = 128
 SINGLES = 4
+HALVES = 2
 
 
 def dot_t(x, y):
@@ -83,51 +84,59 @@
         ref[...] = jnp.zeros_like(ref)
     pl.semaphore_wait(barrier, COLS + ROWS - 1)
 
-    def col_copy(par, slot, at, height, peer):
-        where = col_buf.at[par, slot, pl.ds(0, height)]
+    def col_copy(ch, par, slot, at, height, peer):
+        where = col_buf.at[ch, par, slot, pl.ds(0, height)]
         return pltpu.make_async_remote_copy(
             src_ref=where, dst_ref=where,
-            send_sem=col_send.at[par, at], recv_sem=col_recv.at[par, slot],
+            send_sem=col_send.at[ch, par, at], recv_sem=col_recv.at[ch, par, slot],
             device_id=(layer, row, peer), device_id_type=MESH,
         )
 
-    def row_copy(par, slot, at, height, width, peer):
-        where = row_buf.at[par, slot, pl.ds(0, height), pl.ds(0, width)]
+    def row_copy(ch, par, slot, at, height, width, peer):
+        where = row_buf.at[ch, par, slot, pl.ds(0, height), pl.ds(0, width)]
         return pltpu.make_async_remote_copy(
             src_ref=where, dst_ref=where,
-            send_sem=row_send.at[par, at], recv_sem=row_recv.at[par, slot],
+            send_sem=row_send.at[ch, par, at], recv_sem=row_recv.at[ch, par, slot],
             device_id=(layer, peer, col), device_id_type=MESH,
         )
 
-    def over_col(par, value, beside):
+    def start_col(ch, par, value):
         height = value.shape[0]
-        col_buf[par, col, 0:height] = value
+        col_buf[ch, par, col, 0:height] = value
         for at, peer in enumerate(col_peers):
-            col_copy(par, col, at, height, peer).start()
-        beside()
+            col_copy(ch, par, col, at, height, peer).start()
+
+    def finish_col(ch, par, height):
         for at, peer in enumerate(col_peers):
-            col_copy(par, peer, at, height, peer).wait_recv()
-        total = col_buf[par, 0, 0:height]
+            col_copy(ch, par, peer, at, height, peer).wait_recv()
+        total = col_buf[ch, par, 0, 0:height]
         for slot in range(1, COLS):
-            total = total + col_buf[par, slot, 0:height]
-        for at, peer in enumerate(col_peers):
-            col_copy(par, col, at, height, peer).wait_send()
+            total = total + col_buf[ch, par, slot, 0:height]
         return total
 
-    def over_row(par, value, beside):
+    def drain_col(par, height):
+        for ch in range(HALVES):
+            for at, peer in enumerate(col_peers):
+                col_copy(ch, par, col, at, height, peer).wait_send()
+
+    def start_row(ch, par, value):
         height, width = value.shape
-        row_buf[par, row, 0:height, 0:width] = value
+        row_buf[ch, par, row, 0:height, 0:width] = value
         for at, peer in enumerate(row_peers):
-            row_copy(par, row, at, height, width, peer).start()
-        beside()
+            row_copy(ch, par, row, at, height, width, peer).start()
+
+    def finish_row(ch, par, height, width):
         for at, peer in enumerate(row_peers):
-            row_copy(par, peer, at, height, width, peer).wait_recv()
-        total = row_buf[par, 0, 0:height, 0:width]
+            row_copy(ch, par, peer, at, height, width, peer).wait_recv()
+        total = row_buf[ch, par, 0, 0:height, 0:width]
         for slot in range(1, ROWS):
-            total = total + row_buf[par, slot, 0:height, 0:width]
-        for at, peer in enumerate(row_peers):
-            row_copy(par, row, at, height, width, peer).wait_send()
+            total = total + row_buf[ch, par, slot, 0:height, 0:width]
         return total
+
+    def drain_row(par, height, width):
+        for ch in range(HALVES):
+            for at, peer in enumerate(row_peers):
+                row_copy(ch, par, row, at, height, width, peer).wait_send()
 
     phases = (
         (0, 2, child_wt, child_factor, 2),
@@ -313,83 +322,99 @@
         for at in range(PAIRS):
             lift_buf[at] += dot_t(value, pair_rows(coupling, at, block))
 
-    value = None
-    for block in range(SINGLES):
+    fine = half // HALVES
+    child_rows = [slice(ch * half, (ch + 1) * half) for ch in range(HALVES)]
+    root_rows = [slice(ch * fine, (ch + 1) * fine) for ch in range(HALVES)]
+
+    def child_value(ch, block):
+        value = finish_row(ch, block % 2, half, WIDE)
+        rows, pair, side = child_rows[ch], block // 2, block % 2
+        u_ref[pair, rows, side * WIDE:(side + 1) * WIDE] = value
+        if side == 0:
+            acc_f[pair, rows, THIN:] += dot_t(value, child_factor[block + 1, block])
+        else:
+            acc_f[pair + 1, rows] += dot_t(value, pair_rows(child_factor, pair + 1, block))
+
+    def child_block(block):
+        return u_ref[block // 2, :, (block % 2) * WIDE:(block % 2 + 1) * WIDE]
+
+    loads[0].wait()
+    for ch in range(HALVES):
+        start_row(ch, 0, dot_n(child_rhs[0, child_rows[ch], 0:THIN], child_wt[0]))
+    for load in loads[1:]:
+        load.wait()
+    fill_superw()
+    for block in range(1, SINGLES):
         par = block % 2
         pair, side = block // 2, block % 2
         low, high = side * THIN, (side + 1) * THIN
-
-        def col_work():
-            if block == 1:
-                gather_z(0)
-            if block == 2:
-                in_team(0, gather_xy)
-            if block == 3:
-                in_team(0, second_product)
-            child_trailing(value, block - 1, pair + 1)
-
-        def row_work():
-            if block == 0:
-                loads[1].wait()
-                loads[2].wait()
-                loads[3].wait()
-                loads[4].wait()
-                fill_superw()
-            else:
-                lifting(value, block - 1)
-            if block == 2:
-                in_team(0, first_product)
-            if block == 3:
-                in_team(0, lambda: spread(0))
-                gather_z(1)
-
-        pending = child_rhs[pair, :, low:high]
-        if block == 0:
-            loads[0].wait()
-        else:
-            pending = pending - unpack(over_col(par, pack(acc_f[pair, :, low:high]), col_work))
-        value_now = over_row(par, dot_n(pending, child_wt[block]), row_work)
-        value = value_now
-        u_ref[pair, :, side * WIDE:(side + 1) * WIDE] = value
-        if side == 0:
-            acc_f[pair, :, THIN:] += dot_t(value, child_factor[block + 1, block])
-        else:
-            acc_f[pair + 1] += dot_t(value, pair_rows(child_factor, pair + 1, block))
+        for ch in range(HALVES):
+            child_value(ch, block - 1)
+            start_col(ch, par, pack(acc_f[pair, child_rows[ch], low:high]))
+        if block == 1:
+            gather_z(0)
+        if block == 2:
+            in_team(0, gather_xy)
+        if block == 3:
+            in_team(0, second_product)
+        drain_row(1 - par, half, WIDE)
+        child_trailing(child_block(block - 1), block - 1, pair + 1)
+        for ch in range(HALVES):
+            total = unpack(finish_col(ch, par, half // 2))
+            pending = child_rhs[pair, child_rows[ch], low:high] - total
+            start_row(ch, par, dot_n(pending, child_wt[block]))
+        if block == 2:
+            in_team(0, first_product)
+        if block == 3:
+            in_team(0, lambda: spread(0))
+            gather_z(1)
+        drain_col(par, half // 2)
+        lifting(child_block(block - 1), block - 1)
+
+    def child_pair(ch, pair):
+        value = finish_row(ch, pair % 2, half, 2 * WIDE)
+        rows = child_rows[ch]
+        u_ref[pair, rows] = value
+        if pair + 1 < PAIRS:
+            for side in range(2):
+                acc_f[pair + 1, rows] += dot_t(
+                    value[:, side * WIDE:(side + 1) * WIDE],
+                    pair_rows(child_factor, pair + 1, 2 * pair + side),
+                )
 
     for pair in range(SINGLES // 2, PAIRS):
         par = pair % 2
-
-        def col_work():
-            if pair == SINGLES // 2:
-                in_team(1, gather_xy)
-                child_trailing(value, SINGLES - 1, pair + 1)
-                lifting(value, SINGLES - 1)
+        opening = pair == SINGLES // 2
+        for ch in range(HALVES):
+            if opening:
+                child_value(ch, SINGLES - 1)
             else:
-                for side in range(2):
-                    child_trailing(
-                        value[:, side * WIDE:(side + 1) * WIDE], 2 * pair - 2 + side, pair + 1
-                    )
-                in_team(1, second_product)
-
-        def row_work():
-            if pair == SINGLES // 2:
-                in_team(1, first_product)
-            else:
-                for side in range(2):
-                    lifting(value[:, side * WIDE:(side + 1) * WIDE], 2 * pair - 2 + side)
-                in_team(1, lambda: spread(1))
-
-        pending = child_rhs[pair] - over_col(par, acc_f[pair], col_work)
+                child_pair(ch, pair - 1)
+            start_col(ch, par, acc_f[pair, child_rows[ch]])
+        if opening:
+            in_team(1, gather_xy)
+            drain_row(1 - par, half, WIDE)
+            child_trailing(child_block(SINGLES - 1), SINGLES - 1, pair + 1)
+            lifting(child_block(SINGLES - 1), SINGLES - 1)
+        else:
+            in_team(1, second_product)
+            drain_row(1 - par, half, 2 * WIDE)
+            for block in (2 * pair - 2, 2 * pair - 1):
+                child_trailing(child_block(block), block, pair + 1)
         inverse_ready(pair)
-        value_now = over_row(par, dot_n(pending, superw[pair]), row_work)
-        value = value_now
-        u_ref[pair] = value
-        if pair + 1 < PAIRS:
-            for side in range(2):
-                acc_f[pair + 1] += dot_t(
-                    value[:, side * WIDE:(side + 1) * WIDE],
-                    pair_rows(child_factor, pair + 1, 2 * pair + side),
-                )
+        for ch in range(HALVES):
+            pending = child_rhs[pair, child_rows[ch]] - finish_col(ch, par, half)
+            start_row(ch, par, dot_n(pending, superw[pair]))
+        if opening:
+            in_team(1, first_product)
+        else:
+            in_team(1, lambda: spread(1))
+            for block in (2 * pair - 2, 2 * pair - 1):
+                lifting(child_block(block), block)
+        drain_col(par, half)
+    for ch in range(HALVES):
+        child_pair(ch, PAIRS - 1)
+    value = u_ref[PAIRS - 1]
 
     def lift_copy(at):
         return pltpu.make_async_remote_copy(
@@ -413,50 +438,52 @@
 
     lift_ready(0)
 
+    def root_residual(pair, par):
+        inverse_ready(PAIRS + pair)
+        for ch in range(HALVES):
+            rows = pl.ds(pl.multiple_of(mine + ch * fine, fine), fine)
+            pending = root_rhs[pair, rows] - finish_col(ch, par, fine)
+            start_row(ch, par, dot_n(pending, superw[PAIRS + pair]))
+
+    for ch in range(HALVES):
+        start_col(ch, 0, acc_r[0, root_rows[ch]])
+    drain_row(1, half, 2 * WIDE)
+    for at in range(1, PAIRS):
+        lift_ready(at)
+    root_residual(0, 0)
+    gather_z(2)
+    drain_col(0, fine)
+
     def root_forward(pair, carry):
         par = lax.rem(pair, 2)
-
-        def col_work():
-            @pl.when(pair == 0)
-            def _():
-                for at in range(1, PAIRS):
-                    lift_ready(at)
-
-            @pl.when(pair > 0)
-            def _():
-                before = v_ref[jnp.maximum(pair - 1, 0)]
-
-                @pl.loop(pair + 1, PAIRS)
-                def _(later):
-                    for side in range(2):
-                        acc_r[later] += dot_t(
-                            before[:, side * WIDE:(side + 1) * WIDE],
-                            pair_rows(root_factor, later, 2 * pair - 2 + side),
-                        )
-
-        pending = root_rhs[pair, pl.ds(mine, half)] - over_col(par, acc_r[pair], col_work)
-        inverse_ready(PAIRS + pair)
-
-        def row_work():
-            pl.when(pair == 0)(lambda: gather_z(2))
-            pl.when(pair == 1)(lambda: in_team(2, gather_xy))
-            pl.when(pair == 2)(lambda: in_team(2, first_product))
-            pl.when(pair == 3)(lambda: in_team(2, second_product))
-
-        value = over_row(par, dot_n(pending, superw[PAIRS + pair]), row_work)
-        v_ref[pair] = value
-
-        @pl.when(pair + 1 < PAIRS)
-        def _():
-            for side in range(2):
-                acc_r[pair + 1] += dot_t(
+        for ch in range(HALVES):
+            value = finish_row(ch, 1 - par, fine, 2 * WIDE)
+            v_ref[pair - 1, root_rows[ch]] = value
+            for side in range(2):
+                acc_r[pair, root_rows[ch]] += dot_t(
                     value[:, side * WIDE:(side + 1) * WIDE],
-                    pair_rows(root_factor, pair + 1, 2 * pair + side),
-                )
-
+                    pair_rows(root_factor, pair, 2 * pair - 2 + side),
+                )
+            start_col(ch, par, acc_r[pair, root_rows[ch]])
+        drain_row(1 - par, fine, 2 * WIDE)
+        before = v_ref[pair - 1]
+
+        @pl.loop(pair + 1, PAIRS)
+        def _(later):
+            for side in range(2):
+                acc_r[later] += dot_t(
+                    before[:, side * WIDE:(side + 1) * WIDE],
+                    pair_rows(root_factor, later, 2 * pair - 2 + side),
+                )
+
+        root_residual(pair, par)
+        pl.when(pair == 1)(lambda: in_team(2, gather_xy))
+        pl.when(pair == 2)(lambda: in_team(2, first_product))
+        pl.when(pair == 3)(lambda: in_team(2, second_product))
+        drain_col(par, fine)
         return carry
 
-    lax.fori_loop(0, PAIRS, root_forward, 0)
+    lax.fori_loop(1, PAIRS, root_forward, 0)
 
     def s_copy(pair):
         return pltpu.make_async_remote_copy(
@@ -477,101 +504,110 @@
                 value, pair_rows(coupling, pair, 2 * earlier + side)
             )
 
-    def root_backward(step, first):
+    for ch in range(HALVES):
+        value = finish_row(ch, 1, fine, 2 * WIDE)
+        v_ref[PAIRS - 1, root_rows[ch]] = value
+        start_col(ch, 0, dot_t(value, superw[2 * PAIRS - 1]))
+    in_team(2, lambda: spread(2))
+    drain_row(1, fine, 2 * WIDE)
+
+    def root_backward(step, carry):
         par = lax.rem(step, 2)
         pair = PAIRS - 1 - step
-        after = jnp.minimum(pair + 1, PAIRS - 1)
-
-        def row_work():
-            value = s_half[after]
-
-            @pl.loop(0, pair)
-            def _(earlier):
-                for side in range(2):
-                    acc_b[earlier, :, side * WIDE:(side + 1) * WIDE] += dot_n(
-                        value, pair_rows(root_factor, after, 2 * earlier + side)
-                    )
-
-        def col_work():
-            if first:
-                in_team(2, lambda: spread(2))
-                return
-            root_solved(after)
-            value = root_out[after]
-
-            @pl.loop(0, PAIRS)
-            def _(earlier):
-                lower(value, after, earlier)
-
-        pending = v_ref[pair]
-        if not first:
-            pending = pending - over_row(1 - par, acc_b[pair], row_work)
-        value = over_col(par, dot_t(pending, superw[PAIRS + pair]), col_work)
-        s_half[pair] = value
-        s_copy(pair).start()
-
-        @pl.when(pair > 0)
-        def _():
-            before = jnp.maximum(pair - 1, 0)
-            for side in range(2):
-                acc_b[before, :, side * WIDE:(side + 1) * WIDE] += dot_n(
-                    value, pair_rows(root_factor, pair, 2 * before + side)
-                )
-
-        return 0
-
-    root_backward(jnp.int32(0), True)
-    lax.fori_loop(1, PAIRS, lambda step, carry: root_backward(step, False), 0)
+        after = pair + 1
+        for ch in range(HALVES):
+            rows = root_rows[ch]
+            value = finish_col(ch, 1 - par, fine)
+            s_half[after, rows] = value
+            for side in range(2):
+                acc_b[pair, rows, side * WIDE:(side + 1) * WIDE] += dot_n(
+                    value, pair_rows(root_factor, after, 2 * pair + side)
+                )
+            start_row(ch, 1 - par, acc_b[pair, rows])
+        s_copy(after).start()
+        drain_col(1 - par, fine)
+        solved = s_half[after]
+
+        @pl.loop(0, pair)
+        def _(earlier):
+            for side in range(2):
+                acc_b[earlier, :, side * WIDE:(side + 1) * WIDE] += dot_n(
+                    solved, pair_rows(root_factor, after, 2 * earlier + side)
+                )
+
+        for ch in range(HALVES):
+            pending = v_ref[pair, root_rows[ch]] - finish_row(ch, 1 - par, fine, 2 * WIDE)
+            start_col(ch, par, dot_t(pending, superw[PAIRS + pair]))
+        drain_row(1 - par, fine, 2 * WIDE)
+        root_solved(after)
+        both = root_out[after]
+
+        @pl.loop(0, PAIRS)
+        def _(earlier):
+            lower(both, after, earlier)
+
+        return carry
+
+    lax.fori_loop(1, PAIRS, root_backward, 0)
+    for ch in range(HALVES):
+        s_half[0, root_rows[ch]] = finish_col(ch, 1, fine)
+    s_copy(0).start()
+    drain_col(1, fine)
     root_solved(0)
+
     last = root_out[0]
     lower(last, 0, PAIRS - 1)
+    for ch in range(HALVES):
+        start_row(ch, 1, acc_c[PAIRS - 1, child_rows[ch]])
+    for earlier in range(PAIRS - 1):
+        lower(last, 0, earlier)
     for at in range(SINGLES // 2):
         inverse_ready(at)
+
+    def child_residual(pair, par):
+        for ch in range(HALVES):
+            pending = u_ref[pair, child_rows[ch]] - finish_row(ch, 1 - par, half, 2 * WIDE)
+            start_col(ch, par, dot_t(pending, superw[pair]))
+        drain_row(1 - par, half, 2 * WIDE)
+
+    child_residual(PAIRS - 1, 0)
 
     def child_backward(step, carry):
         par = lax.rem(step, 2)
         pair = PAIRS - 1 - step
-        after = jnp.minimum(pair + 1, PAIRS - 1)
-
-        def row_work():
-            @pl.when(step == 0)
+        after = pair + 1
+        for ch in range(HALVES):
+            rows = child_rows[ch]
+            value = finish_col(ch, 1 - par, half)
+            child_out[after, rows] = value
+            for side in range(2):
+                acc_c[pair, rows, side * WIDE:(side + 1) * WIDE] += dot_n(
+                    value, pair_rows(child_factor, after, 2 * pair + side)
+                )
+            start_row(ch, 1 - par, acc_c[pair, rows])
+        drain_col(1 - par, half)
+        solved = child_out[after]
+
+        @pl.loop(0, pair)
+        def _(earlier):
+            for side in range(2):
+                acc_c[earlier, :, side * WIDE:(side + 1) * WIDE] += dot_n(
+                    solved, pair_rows(child_factor, after, 2 * earlier + side)
+                )
+
+        child_residual(pair, par)
+        for phase in range(3):
+            @pl.when(step == phase + 1)
             def _():
-                for earlier in range(PAIRS - 1):
-                    lower(root_out[0], 0, earlier)
-
-            @pl.when(step > 0)
-            def _():
-                value = child_out[after]
-
-                @pl.loop(0, pair)
-                def _(earlier):
-                    for side in range(2):
-                        acc_c[earlier, :, side * WIDE:(side + 1) * WIDE] += dot_n(
-                            value, pair_rows(child_factor, after, 2 * earlier + side)
-                        )
-
-        def col_work():
-            for phase in range(3):
-                @pl.when(step == phase)
-                def _():
-                    gather_z(phase, True)
-                    in_team(phase, lambda: spread(phase, True))
-
-        pending = u_ref[pair] - over_row(1 - par, acc_c[pair], row_work)
-        value = over_col(par, dot_t(pending, superw[pair]), col_work)
-        child_out[pair] = value
-
-        @pl.when(pair > 0)
-        def _():
-            before = jnp.maximum(pair - 1, 0)
-            for side in range(2):
-                acc_c[before, :, side * WIDE:(side + 1) * WIDE] += dot_n(
-                    value, pair_rows(child_factor, pair, 2 * before + side)
-                )
+                gather_z(phase, True)
+                in_team(phase, lambda: spread(phase, True))
 
         return carry
 
-    lax.fori_loop(0, PAIRS, child_backward, 0)
+    lax.fori_loop(1, PAIRS, child_backward, 0)
+    for ch in range(HALVES):
+        child_out[0, child_rows[ch]] = finish_col(ch, 1, half)
+    drain_col(1, half)
 
 
 def paired(x):
@@ -611,8 +647,8 @@
             pltpu.VMEM((PAIRS, half, 2 * WIDE), f32),
             pltpu.VMEM((PAIRS, nrhs, 2 * WIDE), f32),
             pltpu.VMEM((2 * PAIRS, 2 * THIN, 2 * WIDE), f32),
-            pltpu.VMEM((2, COLS, nrhs, 2 * THIN), f32),
-            pltpu.VMEM((2, ROWS, nrhs, 2 * WIDE), f32),
+            pltpu.VMEM((HALVES, 2, COLS, half, 2 * THIN), f32),
+            pltpu.VMEM((HALVES, 2, ROWS, half, 2 * WIDE), f32),
             pltpu.VMEM((PAIRS, nrhs, 2 * THIN), f32),
             pltpu.VMEM((PAIRS, half, 2 * THIN), f32),
             pltpu.VMEM((4, COLS, THIN, WIDE), f32),
@@ -622,7 +658,8 @@
             pltpu.VMEM((COLS, 4 * THIN, WIDE), f32),
             pltpu.VMEM((4, 2, 4 * THIN, WIDE), f32),
             pltpu.VMEM((2, 4 * THIN, WIDE), f32),
-            dma((2, COLS)), dma((2, COLS)), dma((2, ROWS)), dma((2, ROWS)),
+            dma((HALVES, 2, COLS)), dma((HALVES, 2, COLS)),
+            dma((HALVES, 2, ROWS)), dma((HALVES, 2, ROWS)),
             dma((PAIRS,)), dma((PAIRS,)), dma((PAIRS,)), dma((PAIRS,)),
             dma((3, 2, 3)), dma((3,)), dma((4, 4)), dma((4, 4)),
             dma((2, 2, 4)), dma((2 * PAIRS,)), dma((5,)),

time: 256 us -> 244 us (0.953)
  Pallas kernels: 246 us -> 234 us
    pallas_call x1, Pallas kernels: 246 us -> 234 us  [local(): pl.pallas_call(kernel, out_shape=(jax.ShapeDtypeStruct((PAIRS, nrhs, 2 *...]
where the time goes in v5:
time: 244 us; the launch traced here: 243 us
  Pallas kernels  234 us (96%)
  local copies, waits for them, and re-layouts  8.7 us (4%)
    pallas_call x1, Pallas kernels, local(): pl.pallas_call(kernel, out_shape=(jax.ShapeDtypeStruct((PAIRS, nrhs, 2 *...  234 us
    unnamed x8, local copies, waits for them, and re-layouts  5.08 us

profile of v5, /device:TPU:1, one launch (start us, length us, event | category | flops | bytes accessed | tf_op | source)
XLA Modules:
  0.0 243.3 jit_solution(6231137942158970974)
XLA Ops:
  0.6 1.0 reshape.10
  1.6 1.0 reshape_squeeze.3
  2.7 0.0 copy-start
  2.7 1.6 copy-done
  4.2 0.0 copy-start.1
  4.3 1.6 copy-done.1
  5.8 0.0 copy-start.2
  5.8 0.9 copy-done.2
  6.8 0.0 copy-start.3
  6.8 0.9 copy-done.3
  7.7 234.0 %shard_map.86 = (f32[4,32,128]{2,1,0:T(8,128)S(1)}, f32[4,32,128]{2,1,0:T(8,128)S(1)}) custom-call(f32[4,32,128]{2,1,0:T(8,128)S(1)} %get-tuple-element.7.root_rhs, f32[4,32,128]{2,1,0:T(8,128)S(1)} %get-tuple-element.6.child_rhs, f32[8,8,64,128]{3,2,1,0:T(8,128)S(1)} %copy-done, f32[8,8,64,128]{3,2,1,0:T(8,128)S(1)} %bitcast.14, ...), custom_call_target="tpu_custom_call" | custom-call | tf_op jit(solution)/shard_map/pallas_call | solution.py:627
  241.8 0.8 broadcast_in_dim_reshape.3
  242.6 0.8 reshape.11
  (3 shorter events, 0.1 us)
Async XLA Ops:
  2.7 1.6 copy-start
  4.2 1.6 copy-start.1
  5.8 0.9 copy-start.2
  6.8 0.9 copy-start.3

commit v6 on v5

--- a/solution.py
+++ b/solution.py
@@ -44,8 +44,10 @@
 
 
 def kernel(
-    root_rhs, child_rhs, root_factor_hbm, child_factor_hbm, coupling_hbm, root_wt_hbm, child_wt_hbm,
-    root_out, child_out,
+    root_rhs_in, child_rhs_in, root_factor_hbm, child_factor_hbm, coupling_hbm, root_wt_hbm,
+    child_wt_hbm,
+    root_result, child_result,
+    root_rhs, child_rhs, root_out, child_out,
     root_factor, child_factor, coupling, root_wt, child_wt,
     u_ref, v_ref, s_half, s_in, acc_f, acc_r, acc_b, acc_c, superw,
     col_buf, row_buf, lift_buf, lift_in, a0_buf, c_buf, a1_buf, t_buf, x_out, x_in, x_buf,
@@ -80,6 +82,10 @@
     for peer in row_peers:
         pl.semaphore_signal(barrier, inc=1, device_id=(layer, peer, col), device_id_type=MESH)
     pl.semaphore_signal(barrier, inc=1, device_id=other, device_id_type=MESH)
+    for block in range(2 * PAIRS):
+        at = (block // 2, slice(None), slice((block % 2) * THIN, (block % 2 + 1) * THIN))
+        child_rhs[at] = child_rhs_in[:, block]
+        root_rhs[at] = root_rhs_in[:, block]
     for ref in (acc_f, acc_b, acc_c, lift_buf):
         ref[...] = jnp.zeros_like(ref)
     pl.semaphore_wait(barrier, COLS + ROWS - 1)
@@ -210,7 +216,7 @@
     def in_team(phase, work):
         pl.when(lax.rem(col, 4) == phases[phase][0])(work)
 
-    def gather_xy():
+    def gather_ac():
         arrived(c_buf.at[row4], z_recv.at[1])
         for to in range(4):
             @pl.when(row4 != to)
@@ -224,6 +230,11 @@
                     @pl.when(rowm != to)
                     def _():
                         a0_copy(part, rowm, to).start()
+
+    def gather_a1():
+        for part in range(4):
+            @pl.when(row4 == part)
+            def _():
                 arrived(tail(a1_buf, row4, part), z_recv.at[2])
                 for to in range(4):
                     if to != part:
@@ -257,10 +268,12 @@
             x_out[at] = dot_n(
                 t_buf[:, 0:deep * THIN], a1_buf[0:deep, at].reshape(deep * THIN, WIDE)
             )
-            if at % 2 == 1:
-                @pl.when(rowm != at // 2)
-                def _():
-                    part_copy(rowm, at // 2).start()
+
+    def send_parts():
+        for to in range(4):
+            @pl.when(rowm != to)
+            def _():
+                part_copy(rowm, to).start()
 
     def spread(phase, finish=False):
         if finish:
@@ -343,6 +356,8 @@
         start_row(ch, 0, dot_n(child_rhs[0, child_rows[ch], 0:THIN], child_wt[0]))
     for load in loads[1:]:
         load.wait()
+    gather_z(0)
+    gather_z(1)
     fill_superw()
     for block in range(1, SINGLES):
         par = block % 2
@@ -351,23 +366,24 @@
         for ch in range(HALVES):
             child_value(ch, block - 1)
             start_col(ch, par, pack(acc_f[pair, child_rows[ch], low:high]))
-        if block == 1:
-            gather_z(0)
-        if block == 2:
-            in_team(0, gather_xy)
-        if block == 3:
-            in_team(0, second_product)
+        for phase in range(2):
+            if block == 1:
+                in_team(phase, gather_ac)
+            if block == 2:
+                in_team(phase, gather_a1)
+                in_team(phase, first_product)
+            if block == 3:
+                in_team(phase, lambda: spread(phase))
         drain_row(1 - par, half, WIDE)
         child_trailing(child_block(block - 1), block - 1, pair + 1)
         for ch in range(HALVES):
             total = unpack(finish_col(ch, par, half // 2))
             pending = child_rhs[pair, child_rows[ch], low:high] - total
             start_row(ch, par, dot_n(pending, child_wt[block]))
-        if block == 2:
-            in_team(0, first_product)
-        if block == 3:
-            in_team(0, lambda: spread(0))
-            gather_z(1)
+        for phase in range(2):
+            if block == 2:
+                in_team(phase, second_product)
+                in_team(phase, send_parts)
         drain_col(par, half // 2)
         lifting(child_block(block - 1), block - 1)
 
@@ -392,12 +408,10 @@
                 child_pair(ch, pair - 1)
             start_col(ch, par, acc_f[pair, child_rows[ch]])
         if opening:
-            in_team(1, gather_xy)
             drain_row(1 - par, half, WIDE)
             child_trailing(child_block(SINGLES - 1), SINGLES - 1, pair + 1)
             lifting(child_block(SINGLES - 1), SINGLES - 1)
         else:
-            in_team(1, second_product)
             drain_row(1 - par, half, 2 * WIDE)
             for block in (2 * pair - 2, 2 * pair - 1):
                 child_trailing(child_block(block), block, pair + 1)
@@ -405,10 +419,7 @@
         for ch in range(HALVES):
             pending = child_rhs[pair, child_rows[ch]] - finish_col(ch, par, half)
             start_row(ch, par, dot_n(pending, superw[pair]))
-        if opening:
-            in_team(1, first_product)
-        else:
-            in_team(1, lambda: spread(1))
+        if not opening:
             for block in (2 * pair - 2, 2 * pair - 1):
                 lifting(child_block(block), block)
         drain_col(par, half)
@@ -465,6 +476,9 @@
                     pair_rows(root_factor, pair, 2 * pair - 2 + side),
                 )
             start_col(ch, par, acc_r[pair, root_rows[ch]])
+        pl.when(pair == 1)(lambda: in_team(2, gather_ac))
+        pl.when(pair == 2)(lambda: in_team(2, gather_a1))
+        pl.when(pair == 3)(lambda: in_team(2, send_parts))
         drain_row(1 - par, fine, 2 * WIDE)
         before = v_ref[pair - 1]
 
@@ -477,9 +491,9 @@
                 )
 
         root_residual(pair, par)
-        pl.when(pair == 1)(lambda: in_team(2, gather_xy))
-        pl.when(pair == 2)(lambda: in_team(2, first_product))
-        pl.when(pair == 3)(lambda: in_team(2, second_product))
+        pl.when(pair == 1)(lambda: in_team(2, first_product))
+        pl.when(pair == 2)(lambda: in_team(2, second_product))
+        pl.when(pair == 3)(lambda: in_team(2, lambda: spread(2)))
         drain_col(par, fine)
         return carry
 
@@ -508,7 +522,6 @@
         value = finish_row(ch, 1, fine, 2 * WIDE)
         v_ref[PAIRS - 1, root_rows[ch]] = value
         start_col(ch, 0, dot_t(value, superw[2 * PAIRS - 1]))
-    in_team(2, lambda: spread(2))
     drain_row(1, fine, 2 * WIDE)
 
     def root_backward(step, carry):
@@ -572,6 +585,13 @@
 
     child_residual(PAIRS - 1, 0)
 
+    def write_pair(result, source, pair):
+        for side in range(2):
+            result[:, 2 * pair + side] = source[pair, :, side * THIN:(side + 1) * THIN]
+
+    for pair in range(PAIRS):
+        write_pair(root_result, root_out, pair)
+
     def child_backward(step, carry):
         par = lax.rem(step, 2)
         pair = PAIRS - 1 - step
@@ -607,15 +627,9 @@
     lax.fori_loop(1, PAIRS, child_backward, 0)
     for ch in range(HALVES):
         child_out[0, child_rows[ch]] = finish_col(ch, 1, half)
+    for pair in range(PAIRS):
+        write_pair(child_result, child_out, pair)
     drain_col(1, half)
-
-
-def paired(x):
-    return jnp.transpose(x.reshape(x.shape[0], PAIRS, 2 * THIN), (1, 0, 2))
-
-
-def unpaired(x):
-    return jnp.transpose(x, (1, 0, 2)).reshape(x.shape[1], 2 * PAIRS, THIN)
 
 
 def local(root_rhs, child_rhs, root_factor, child_factor, coupling, root_inverse, child_inverse):
@@ -627,12 +641,16 @@
     root, child = pl.pallas_call(
         kernel,
         out_shape=(
-            jax.ShapeDtypeStruct((PAIRS, nrhs, 2 * THIN), f32),
-            jax.ShapeDtypeStruct((PAIRS, nrhs, 2 * THIN), f32),
+            jax.ShapeDtypeStruct((nrhs, 2 * PAIRS, THIN), f32),
+            jax.ShapeDtypeStruct((nrhs, 2 * PAIRS, THIN), f32),
         ),
         in_specs=[vmem] * 2 + [pl.BlockSpec(memory_space=pltpu.HBM)] * 5,
         out_specs=[vmem] * 2,
         scratch_shapes=[
+            pltpu.VMEM((PAIRS, nrhs, 2 * THIN), f32),
+            pltpu.VMEM((PAIRS, nrhs, 2 * THIN), f32),
+            pltpu.VMEM((PAIRS, nrhs, 2 * THIN), f32),
+            pltpu.VMEM((PAIRS, nrhs, 2 * THIN), f32),
             pltpu.VMEM(root_factor.shape, f32),
             pltpu.VMEM(root_factor.shape, f32),
             pltpu.VMEM(root_factor.shape, f32),
@@ -665,14 +683,14 @@
             dma((2, 2, 4)), dma((2 * PAIRS,)), dma((5,)),
         ],
         compiler_params=pltpu.CompilerParams(
-            collective_id=0, has_side_effects=True, vmem_limit_bytes=48 << 20
+            collective_id=0, has_side_effects=True, vmem_limit_bytes=60 << 20
         ),
     )(
-        paired(root_rhs), paired(child_rhs[0]),
+        root_rhs, child_rhs[0],
         root_factor, child_factor[0], coupling[0],
         jnp.swapaxes(root_inverse, 1, 2), jnp.swapaxes(child_inverse[0], 1, 2),
     )
-    return unpaired(root), unpaired(child)[None]
+    return root, child[None]
 
 
 def solution(mesh):

time: 244 us -> 237 us (0.971)
  local copies, waits for them, and re-layouts: 8.7 us -> 3.14 us
    unnamed x8 -> x2, local copies, waits for them, and re-layouts: 5.08 us -> 3.14 us
where the time goes in v6:
time: 237 us
  Pallas kernels  233 us (98%)
  local copies, waits for them, and re-layouts  3.14 us (1%)
    pallas_call x1, Pallas kernels, local(): pl.pallas_call(kernel, out_shape=(jax.ShapeDtypeStruct((nrhs, 2 * PAIRS,...  233 us

profile of v6, /device:TPU:1, one launch (start us, length us, event | category | flops | bytes accessed | tf_op | source)
XLA Modules:
  0.0 237.0 jit_solution(15460152753878533124)
XLA Ops:
  0.6 233.2 %shard_map.86 = (f32[32,8,64]{2,1,0:T(8,128)}, f32[32,8,64]{2,1,0:T(8,128)}) custom-call(f32[32,8,64]{2,1,0:T(8,128)} %root_rhs_in.1, f32[32,8,64]{2,1,0:T(8,128)} %bitcast.12, f32[8,8,64,128]{3,2,1,0:T(8,128)} %root_factor_hbm.1, f32[8,8,64,128]{3,2,1,0:T(8,128)} %bitcast.8, f32[8,8,64,128]{3,2,1,0:T(8,128)} %bitcast.9, f32[8,64,128]{2,1,0:T(8,128)} %bitcast.10, ...), custom_call_target="tpu_custom_call" | custom-call | tf_op jit(solution)/shard_map/pallas_call | solution.py:641
  233.9 1.6 copy.11
  235.4 1.6 copy.12

commit v7 on v6

--- a/solution.py
+++ b/solution.py
@@ -15,18 +15,26 @@
 HALVES = 2
 
 
+def halves(x):
+    high = x.astype(jnp.bfloat16)
+    return high, (x - high.astype(jnp.float32)).astype(jnp.bfloat16)
+
+
+def product(x, y, dims):
+    (x_high, x_low), (y_high, y_low) = halves(x), halves(y)
+
+    def one(left, right):
+        return lax.dot_general(left, right, (dims, ((), ())), preferred_element_type=jnp.float32)
+
+    return one(x_high, y_high) + (one(x_high, y_low) + one(x_low, y_high))
+
+
 def dot_t(x, y):
-    return lax.dot_general(
-        x, y, (((1,), (1,)), ((), ())), precision=lax.Precision.HIGHEST,
-        preferred_element_type=jnp.float32,
-    )
+    return product(x, y, ((1,), (1,)))
 
 
 def dot_n(x, y):
-    return lax.dot_general(
-        x, y, (((1,), (0,)), ((), ())), precision=lax.Precision.HIGHEST,
-        preferred_element_type=jnp.float32,
-    )
+    return product(x, y, ((1,), (0,)))
 
 
 def pack(x):

time: 237 us -> 232 us (0.979)
  Pallas kernels: 233 us -> 228 us
    pallas_call x1, Pallas kernels: 233 us -> 228 us  [local(): pl.pallas_call(kernel, out_shape=(jax.ShapeDtypeStruct((nrhs, 2 * PAIRS,...]
where the time goes in v7:
time: 232 us
  Pallas kernels  228 us (98%)
  local copies, waits for them, and re-layouts  3.14 us (1%)
    pallas_call x1, Pallas kernels, local(): pl.pallas_call(kernel, out_shape=(jax.ShapeDtypeStruct((nrhs, 2 * PAIRS,...  228 us

profile of v7, /device:TPU:1, one launch (start us, length us, event | category | flops | bytes accessed | tf_op | source)
XLA Modules:
  0.0 232.1 jit_solution(6945541636388496350)
XLA Ops:
  0.6 228.4 %shard_map.86 = (f32[32,8,64]{2,1,0:T(8,128)}, f32[32,8,64]{2,1,0:T(8,128)}) custom-call(f32[32,8,64]{2,1,0:T(8,128)} %root_rhs_in.1, f32[32,8,64]{2,1,0:T(8,128)} %bitcast.12, f32[8,8,64,128]{3,2,1,0:T(8,128)} %root_factor_hbm.1, f32[8,8,64,128]{3,2,1,0:T(8,128)} %bitcast.8, f32[8,8,64,128]{3,2,1,0:T(8,128)} %bitcast.9, f32[8,64,128]{2,1,0:T(8,128)} %bitcast.10, ...), custom_call_target="tpu_custom_call" | custom-call | tf_op jit(solution)/shard_map/pallas_call | solution.py:649
  229.0 1.6 copy.11
  230.6 1.6 copy.12

commit v8 on v7

--- a/solution.py
+++ b/solution.py
@@ -67,8 +67,12 @@
     col = lax.axis_index("col")
     other = (1 - layer, row, col)
     col_peers = [lax.rem(col + k, COLS) for k in range(1, COLS)]
-    row_peers = [lax.rem(row + k, ROWS) for k in range(1, ROWS)]
     row4, rowm = row // 4, lax.rem(row, 4)
+    offsets = sorted(
+        ((y, x) for y in range(4) for x in range(4) if y or x),
+        key=lambda at: -(min(at[0], 4 - at[0]) + min(at[1], 4 - at[1])),
+    )
+    row_peers = [4 * lax.rem(row4 + y, 4) + lax.rem(rowm + x, 4) for y, x in offsets]
     col2, colm = col // 2, lax.rem(col, 2)
     nrhs = child_rhs.shape[1]
     half = nrhs // 2

time: 232 us -> 229 us (0.987)
  Pallas kernels: 228 us -> 225 us
    pallas_call x1, Pallas kernels: 228 us -> 225 us  [local(): pl.pallas_call(kernel, out_shape=(jax.ShapeDtypeStruct((nrhs, 2 * PAIRS,...]
where the time goes in v8:
time: 229 us
  Pallas kernels  225 us (98%)
  local copies, waits for them, and re-layouts  3.14 us (1%)
    pallas_call x1, Pallas kernels, local(): pl.pallas_call(kernel, out_shape=(jax.ShapeDtypeStruct((nrhs, 2 * PAIRS,...  225 us

profile of v8, /device:TPU:1, one launch (start us, length us, event | category | flops | bytes accessed | tf_op | source)
XLA Modules:
  0.0 228.9 jit_solution(10367821781625936740)
XLA Ops:
  0.6 225.2 %shard_map.86 = (f32[32,8,64]{2,1,0:T(8,128)}, f32[32,8,64]{2,1,0:T(8,128)}) custom-call(f32[32,8,64]{2,1,0:T(8,128)} %root_rhs_in.1, f32[32,8,64]{2,1,0:T(8,128)} %bitcast.12, f32[8,8,64,128]{3,2,1,0:T(8,128)} %root_factor_hbm.1, f32[8,8,64,128]{3,2,1,0:T(8,128)} %bitcast.8, f32[8,8,64,128]{3,2,1,0:T(8,128)} %bitcast.9, f32[8,64,128]{2,1,0:T(8,128)} %bitcast.10, ...), custom_call_target="tpu_custom_call" | custom-call | tf_op jit(solution)/shard_map/pallas_call | solution.py:653
  225.8 1.6 copy.11
  227.4 1.6 copy.12
